TPU v7x, 256 devices: a whole 4x4x8 slice. The times are simulated.
256 devices in a mesh: row: 32 (over z, x), col: 8 (over y, core).
Axes of the slice: x: 4, y: 4, z: 8, core: 2. Of those that a mesh axis runs over, the one named last changes fastest.
Arguments:
- panel_transposed: float32 [256, 65536], P('col', 'row'), may hold values from -0.0234375 to 0.0234375
- trailing: float32 [65536, 4096], P('row', 'col'), may hold values from -6 to 6
Outputs:
- stop_factors: float32 [8192, 256], P('row')
- stop_blocks: float32 [8192, 4096], P('row', 'col')
- projected: float32 [65536, 4096], P('row', 'col')
All inputs are finite; a program needn't handle non-finite values.
Results may differ from a plain program's by a relative error of at most 0.00026.
Values sent between devices are 32-bit elements; how exact they have to be, the bound alone decides.
No kernel may reach another device: no remote copies, remote signals or barrier semaphores. Data moves between devices by JAX's collectives and lax.ppermute only.
A program may use at most 128 MiB of HBM per device.

v0:
```python
import jax
import jax.numpy as jnp
from jax import lax
from jax.experimental import pallas as pl
from jax.experimental.pallas import tpu as pltpu
from jax.sharding import PartitionSpec as P


HIGHEST = lax.Precision.HIGHEST
F32 = jnp.float32
BF16 = jnp.bfloat16
X = 4


def dot(left, right, dims=(1, 0), precision=HIGHEST):
    return lax.dot_general(
        left,
        right,
        (((dims[0],), (dims[1],)), ((), ())),
        precision=precision,
        preferred_element_type=F32,
    )


def halves(value):
    high = value.astype(BF16)
    return high, (value - high.astype(F32)).astype(BF16)


def dot3(left, right, dims=(1, 0)):
    (lh, ll), (rh, rl) = left, right
    default = lax.Precision.DEFAULT
    return dot(lh, rh, dims, default) + (dot(ll, rh, dims, default) + dot(lh, rl, dims, default))


def room(mebibytes):
    return pltpu.CompilerParams(vmem_limit_bytes=mebibytes * 2**20)


def cost(us):
    return pl.CostEstimate(flops=int(us * 5e8), bytes_accessed=int(us * 1e6), transcendentals=0)


def rotate(value, axis, pairs):
    return lax.ppermute(value, axis, pairs)


def from_chips(value):
    count = lax.axis_size("col")
    sames = [value] + [
        rotate(value, "col", [(i, (i + 2 * k) % count) for i in range(count)]) for k in (1, 3, 2)
    ]
    others = [rotate(v, "col", [(i, i ^ 1) for i in range(count)]) for v in sames]
    return sames + others


def chip_offsets():
    me = lax.axis_index("col")
    count = lax.axis_size("col")
    chip, core = me // 2, lax.rem(me, 2)
    chips = count // 2
    steps = (0, 1, 3, 2)
    return [2 * lax.rem(chip + chips - k, chips) + (core if same else 1 - core) for same in (True, False) for k in steps]


def from_stops_x(value):
    count = lax.axis_size("row")
    return [
        rotate(value, "row", [(i, i - i % X + (i + k) % X) for i in range(count)]) for k in (1, 3, 2)
    ]


def from_pair_z(value):
    count = lax.axis_size("row")
    return rotate(value, "row", [(i, i ^ X) for i in range(count)])


def from_pairs_z(value):
    count = lax.axis_size("row")
    return [rotate(value, "row", [(i, (i + 2 * X * k) % count) for i in range(count)]) for k in (1, 3, 2)]


def gather_kernel(*refs):
    pieces, (high_ref, low_ref, gram_ref, whole_ref) = refs[:-4], refs[-4:]
    height = pieces[0].shape[0]
    for piece, owner in zip(pieces, chip_offsets()):
        rows = pl.ds(pl.multiple_of(owner * height, height), height)
        value = piece[...]
        whole_ref[rows, :] = value
        high, low = halves(value)
        high_ref[rows, :] = high
        low_ref[rows, :] = low
    gram_ref[...] = dot(pieces[0][...], whole_ref[...], (1, 1))


def gather(pieces):
    height, rows = pieces[0].shape
    width = height * len(pieces)
    shapes = [(width, rows, BF16), (width, rows, BF16), (height, width, F32)]
    return pl.pallas_call(
        gather_kernel,
        out_shape=[jax.ShapeDtypeStruct((a, b), t) for a, b, t in shapes],
        scratch_shapes=[pltpu.VMEM((width, rows), F32)],
        cost_estimate=cost(4),
        compiler_params=room(16),
        name="gather",
    )(*pieces)


def turn_kernel(high_ref, low_ref, high_out, low_out):
    high_out[...] = high_ref[...].T
    low_out[...] = low_ref[...].T


def turn(high, low):
    width, rows = high.shape
    block = 512
    shape = pltpu.HBM((rows, width), BF16)
    return pl.pallas_call(
        turn_kernel,
        grid=(rows // block,),
        in_specs=[pl.BlockSpec((width, block), lambda i: (0, i))] * 2,
        out_specs=[pl.BlockSpec((block, width), lambda i: (i, 0))] * 2,
        out_shape=[shape, shape],
        cost_estimate=cost(3),
        compiler_params=room(8),
        name="turn",
    )(high, low)


def cross_kernel(high_ref, low_ref, trailing_ref, out_ref):
    @pl.when(pl.program_id(0) == 0)
    def _():
        out_ref[...] = jnp.zeros_like(out_ref)

    out_ref[...] += dot3((high_ref[...], low_ref[...]), halves(trailing_ref[...]))


def cross(high, low, trailing):
    width, rows = high.shape
    columns = trailing.shape[1]
    block = 512
    return pl.pallas_call(
        cross_kernel,
        grid=(rows // block,),
        in_specs=[
            pl.BlockSpec((width, block), lambda i: (0, i)),
            pl.BlockSpec((width, block), lambda i: (0, i)),
            pl.BlockSpec((block, columns), lambda i: (i, 0)),
        ],
        out_specs=pl.BlockSpec((width, columns), lambda i: (0, 0)),
        out_shape=jax.ShapeDtypeStruct((width, columns), F32),
        cost_estimate=cost(5),
        compiler_params=room(16),
        name="cross",
    )(high, low, trailing)


def group_kernel(own_ref, one_ref, three_ref, two_ref, prefix_ref, total_ref):
    place = lax.rem(lax.axis_index("row"), X)
    own, one, two, three = own_ref[...], one_ref[...], two_ref[...], three_ref[...]
    prefix_ref[...] = (
        own + jnp.where(place >= 1, one, 0.0) + jnp.where(place >= 2, two, 0.0) + jnp.where(place >= 3, three, 0.0)
    )
    total_ref[...] = (own + one) + (two + three)


def pair_kernel(before_ref, total_ref, other_ref, prefix_ref, pair_ref):
    odd = lax.rem(lax.div(lax.axis_index("row"), X), 2)
    other = other_ref[...]
    prefix_ref[...] = before_ref[...] + jnp.where(odd == 1, other, 0.0)
    pair_ref[...] = total_ref[...] + other


def pairs_kernel(before_ref, own_ref, one_ref, three_ref, two_ref, out_ref):
    place = lax.div(lax.axis_index("row"), 2 * X)
    own, one, two, three = own_ref[...], one_ref[...], two_ref[...], three_ref[...]
    out_ref[0] = (
        before_ref[...]
        + jnp.where(place >= 1, one, 0.0)
        + jnp.where(place >= 2, two, 0.0)
        + jnp.where(place >= 3, three, 0.0)
    )
    out_ref[1] = (own + one) + (two + three)


def small(kernel, shapes, *values):
    return pl.pallas_call(
        kernel,
        out_shape=[jax.ShapeDtypeStruct(shape, F32) for shape in shapes],
        cost_estimate=cost(1),
        compiler_params=room(2),
    )(*values)


def scan_kernel(pieces_ref, out_ref):
    stops, height, _ = pieces_ref.shape
    total = pieces_ref[0]
    out_ref[0, :height] = total
    for s in range(1, stops):
        total = total + pieces_ref[s]
        out_ref[s, :height] = total
    for s in range(stops):
        out_ref[s, height:] = total


def scan(pieces):
    stops, height, columns = pieces.shape
    return pl.pallas_call(
        scan_kernel,
        out_shape=jax.ShapeDtypeStruct((stops, 2 * height, columns), F32),
        cost_estimate=cost(1),
        compiler_params=room(4),
        name="scan",
    )(pieces)


def eliminate(matrices):
    order = matrices[0].shape[0]
    count = order // 8
    full = (8, order)
    lane = lax.broadcasted_iota(jnp.int32, full, 1)
    sublane = lax.broadcasted_iota(jnp.int32, full, 0)
    grids = [[m[8 * g : 8 * g + 8, :] for g in range(count)] for m in matrices]
    for p in range(count):
        start = 8 * p
        inside = (lane >= start) & (lane < start + 8)
        for grid in grids:
            block = grid[p]
            columns = [jnp.broadcast_to(block[:, start + c : start + c + 1], full) for c in range(8)]
            entry = [[None] * r + [jnp.broadcast_to(columns[r][c : c + 1, :], full) for c in range(r, 8)] for r in range(8)]
            rows = [jnp.broadcast_to(block[r : r + 1, :], full) for r in range(8)]
            rows = [jnp.where(inside, jnp.where(lane == start + r, 1.0, 0.0), rows[r]) for r in range(8)]
            inverse, multiple = [], [[None] * 8 for _ in range(8)]
            for k in range(8):
                inverse.append(1.0 / entry[k][k])
                for r in range(k + 1, 8):
                    multiple[r][k] = entry[k][r] * inverse[k]
                for r in range(k + 1, 8):
                    for c in range(r, 8):
                        entry[r][c] = entry[r][c] - multiple[r][k] * entry[k][c]
                    rows[r] = rows[r] - multiple[r][k] * rows[k]
            result = rows[0]
            for r in range(1, 8):
                result = jnp.where(sublane == r, rows[r], result)
            for c in range(8):
                column = entry[0][c]
                for r in range(1, c + 1):
                    column = jnp.where(sublane == r, entry[r][c], column)
                result = jnp.where((lane == start + c) & (sublane <= c), column, result)
            if p < count - 1:
                solved = [rows[k] * inverse[k] for k in range(8)]
                for k in range(6, -1, -1):
                    for r in range(k + 1, 8):
                        solved[k] = solved[k] - multiple[r][k] * solved[r]
                for g in range(p + 1, count):
                    value = jnp.where(inside, 0.0, grid[g])
                    for k in range(8):
                        value = value - jnp.broadcast_to(grid[g][:, start + k : start + k + 1], full) * solved[k]
                    grid[g] = value
            grid[p] = result
    return [jnp.concatenate(grid, 0) for grid in grids]


def split(reduced):
    order = reduced.shape[0]
    row = lax.broadcasted_iota(jnp.int32, (order, order), 0)
    column = lax.broadcasted_iota(jnp.int32, (order, order), 1)
    pivots = jnp.sum(jnp.where(row == column, reduced, 0.0), axis=1, keepdims=True)
    scale = lax.rsqrt(pivots)
    upper = jnp.where(row <= column, reduced, 0.0) * scale
    lower = jnp.where(row > column, reduced, jnp.where(row == column, 1.0, 0.0)) * scale
    return upper, lower


def factor_kernel(*refs):
    pieces, (upper_ref, high_ref, low_ref, gram_ref, inverse_ref) = refs[:-5], refs[-5:]
    count, height, order = pieces[0].shape
    half = order // 2
    for piece, owner in zip(pieces, chip_offsets()):
        gram_ref[:, pl.ds(pl.multiple_of(owner * height, height), height), :] = piece[...]
    tops = eliminate([gram_ref[i, :half, :half] for i in range(count)])
    schurs, sides = [], []
    for i, reduced in enumerate(tops):
        upper, inverse = split(reduced)
        across = dot(inverse, gram_ref[i, :half, half:])
        side = dot(gram_ref[i, half:, :half], inverse, (1, 1))
        schurs.append(gram_ref[i, half:, half:] - dot(side, across))
        sides.append(dot(side, inverse))
        if i == 0:
            upper_ref[:half, :half] = upper
            upper_ref[:half, half:] = across
            upper_ref[half:, :half] = jnp.zeros((half, half), F32)
        inverse_ref[i, :half, :half] = inverse
        inverse_ref[i, :half, half:] = jnp.zeros((half, half), F32)
    for i, reduced in enumerate(eliminate(schurs)):
        upper, inverse = split(reduced)
        if i == 0:
            upper_ref[half:, half:] = upper
        inverse_ref[i, half:, half:] = inverse
        inverse_ref[i, half:, :half] = -dot(inverse, sides[i])
    high_ref[0], low_ref[0] = halves(inverse_ref[0])
    last = inverse_ref[1]
    high_ref[1], low_ref[1] = halves(dot(last, last, (0, 0)))


def factor(pieces):
    count, _, order = pieces[0].shape
    return pl.pallas_call(
        factor_kernel,
        out_shape=[
            jax.ShapeDtypeStruct((order, order), F32),
            pltpu.HBM((count, order, order), BF16),
            pltpu.HBM((count, order, order), BF16),
        ],
        scratch_shapes=[pltpu.VMEM((count, order, order), F32)] * 2,
        cost_estimate=cost(16),
        compiler_params=room(8),
        name="factor",
    )(*pieces)


def project_kernel(sh_ref, sl_ref, sums_ref, high_ref, low_ref, trailing_ref, blocks_ref, out_ref, ch_ref, cl_ref):
    stops, both, columns = sums_ref.shape
    height = both // 2

    @pl.when(pl.program_id(0) == 0)
    def _():
        total = sums_ref[:, height:, :].reshape(stops * height, columns)
        high, low = halves(dot3((sh_ref[1], sl_ref[1]), halves(total)))
        ch_ref[...] = high
        cl_ref[...] = low
        prefix = sums_ref[:, :height, :].reshape(stops * height, columns)
        blocks_ref[...] = dot3((sh_ref[0], sl_ref[0]), halves(prefix))

    out_ref[...] = trailing_ref[...] - dot3((high_ref[...], low_ref[...]), (ch_ref[...], cl_ref[...]))


def in_hbm(value):
    return pltpu.with_memory_space_constraint(value, pltpu.HBM)


def project(solves, sums, high, low, trailing):
    rows, columns = trailing.shape
    width = high.shape[1]
    block = 256
    whole = pl.BlockSpec(solves[0].shape, lambda i: (0, 0, 0))
    return pl.pallas_call(
        project_kernel,
        grid=(rows // block,),
        in_specs=[
            whole,
            whole,
            pl.BlockSpec(sums.shape, lambda i: (0, 0, 0)),
            pl.BlockSpec((block, width), lambda i: (i, 0)),
            pl.BlockSpec((block, width), lambda i: (i, 0)),
            pl.BlockSpec((block, columns), lambda i: (i, 0)),
        ],
        out_specs=[
            pl.BlockSpec((width, columns), lambda i: (0, 0)),
            pl.BlockSpec((block, columns), lambda i: (i, 0)),
        ],
        out_shape=[
            jax.ShapeDtypeStruct((width, columns), F32),
            jax.ShapeDtypeStruct((rows, columns), F32),
        ],
        scratch_shapes=[pltpu.VMEM((width, columns), BF16)] * 2,
        cost_estimate=cost(8),
        compiler_params=room(16),
        name="project",
    )(*[in_hbm(s) for s in solves], sums, in_hbm(high), in_hbm(low), in_hbm(trailing))


def stages(panel_transposed, trailing):
    stops = lax.axis_size("row")
    high, low, own_gram = gather(from_chips(panel_transposed))
    width = high.shape[0]
    columns = trailing.shape[1]
    piece = own_gram.shape

    def exchange(value):
        return lax.all_to_all(value, "row", 0, 0, tiled=True)

    behind = from_stops_x(own_gram)
    own_cross = cross(high, low, trailing)
    pieces = exchange(own_cross.reshape(stops, width // stops, columns))

    prefix, total = small(group_kernel, [piece] * 2, own_gram, *behind)
    other = from_pair_z(total)
    prefix, total = small(pair_kernel, [piece] * 2, prefix, total, other)
    behind = from_pairs_z(total)
    (grams,) = small(pairs_kernel, [(2,) + piece], prefix, total, *behind)
    grams = from_chips(grams)
    high, low = turn(high, low)

    both = scan(pieces)
    sums = exchange(both)
    grams, both = lax.optimization_barrier((grams, both))
    stop_factors, *solves = factor(grams)
    stop_blocks, projected = project(solves, sums, high, low, trailing)
    return (stop_factors, stop_blocks, projected)


def solution(mesh):
    return jax.shard_map(
        stages,
        mesh=mesh,
        in_specs=(P("col", "row"), P("row", "col")),
        out_specs=(P("row", None), P("row", "col"), P("row", "col")),
        check_vma=False,
    )
```

profile of v0, /device:TPU:1, one launch (start us, length us, event | category | flops | bytes accessed | tf_op | source)
XLA Modules:
  0.0 132.2 jit_solution(7839100072779385965)
XLA Ops:
  0.6 3.8 %collective-permute-start.2 = (f32[32,2048]{1,0:T(8,128)}, f32[32,2048]{1,0:T(8,128)S(1)}, u32[]{:S(2)}, u32[]{:S(2)}) collective-permute-start(f32[32,2048]{1,0:T(8,128)} %refs_0_.1), channel_id=1, source_target_pairs={{0,4},{1,5},{2,6},{3,7},{4,0},{5,1},{6,2},{7,3},{8,12},{9,13},{10,... | collective-permute-start | bytes 786440 | tf_op jit(solution)/shard_map/ppermute | solution.py:45
  5.9 1.5 %collective-permute-start.3 = (f32[32,2048]{1,0:T(8,128)}, f32[32,2048]{1,0:T(8,128)S(1)}, u32[]{:S(2)}, u32[]{:S(2)}) collective-permute-start(f32[32,2048]{1,0:T(8,128)} %refs_0_.1), channel_id=1, source_target_pairs={{0,1},{1,0},{2,3},{3,2},{4,5},{5,4},{6,7},{7,6},{8,9},{9,8},{10,11... | collective-permute-start | bytes 786440 | tf_op jit(solution)/shard_map/ppermute | solution.py:45
  7.4 2.4 %collective-permute-done.2.refs_3_ = f32[32,2048]{1,0:T(8,128)S(1)} collective-permute-done((f32[32,2048]{1,0:T(8,128)}, f32[32,2048]{1,0:T(8,128)S(1)}, u32[]{:S(2)}, u32[]{:S(2)}) %collective-permute-start.2) | collective-permute-done | bytes 262176 | tf_op jit(solution)/shard_map/ppermute | solution.py:45
  9.8 5.0 %collective-permute-start.6 = (f32[32,2048]{1,0:T(8,128)S(1)}, f32[32,2048]{1,0:T(8,128)S(1)}, u32[]{:S(2)}, u32[]{:S(2)}) collective-permute-start(f32[32,2048]{1,0:T(8,128)S(1)} %collective-permute-done.2.refs_3_), channel_id=1, source_target_pairs={{0,1},{1,0},{2,3},{3,2},{4,5},{5,4},{6,7},{7,6},{8,9},{9,8},{10,11... | collective-permute-start | bytes 786440 | tf_op jit(solution)/shard_map/ppermute | solution.py:45
  14.8 1.7 %collective-permute-done.1.refs_2_ = f32[32,2048]{1,0:T(8,128)S(1)} collective-permute-done((f32[32,2048]{1,0:T(8,128)}, f32[32,2048]{1,0:T(8,128)S(1)}, u32[]{:S(2)}, u32[]{:S(2)}) %collective-permute-start.1) | collective-permute-done | bytes 262176 | tf_op jit(solution)/shard_map/ppermute | solution.py:45
  16.5 1.4 %collective-permute-start.5 = (f32[32,2048]{1,0:T(8,128)S(1)}, f32[32,2048]{1,0:T(8,128)S(1)}, u32[]{:S(2)}, u32[]{:S(2)}) collective-permute-start(f32[32,2048]{1,0:T(8,128)S(1)} %collective-permute-done.1.refs_2_), channel_id=1, source_target_pairs={{0,1},{1,0},{2,3},{3,2},{4,5},{5,4},{6,7},{7,6},{8,9},{9,8},{10,11... | collective-permute-start | bytes 786440 | tf_op jit(solution)/shard_map/ppermute | solution.py:45
  18.0 1.1 collective-permute-done.5.refs_6_
  19.5 0.9 copy-done.1
  20.5 2.5 %gather.1 = (bf16[256,2048]{1,0:T(8,128)(2,1)S(1)}, bf16[256,2048]{1,0:T(8,128)(2,1)S(1)}, f32[32,256]{1,0:T(8,128)S(1)}) custom-call(f32[32,2048]{1,0:T(8,128)S(1)} %copy-done.1, f32[32,2048]{1,0:T(8,128)S(1)} %collective-permute-done.refs_1_, f32[32,2048]{1,0:T(8,128)S(1)} %collective-permute-done.1.refs_2_, ...), custom_call_target="tpu_custom_call" | custom-call | flops 2000000000 | bytes 4000000 | tf_op jit(solution)/shard_map/gather/pallas_call | solution.py:100
  23.0 2.6 %cross.1 = f32[256,512]{1,0:T(8,128)S(1)} custom-call(bf16[256,2048]{1,0:T(8,128)(2,1)S(1)} %get-tuple-element.30.high_ref, bf16[256,2048]{1,0:T(8,128)(2,1)S(1)} %get-tuple-element.31.low_ref, f32[2048,512]{1,0:T(8,128)S(1)} %copy-done), custom_call_target="tpu_custom_call" | custom-call | flops 2500000000 | bytes 5000000 | tf_op jit(solution)/shard_map/cross/pallas_call | solution.py:143
  25.7 27.5 %all_to_all.10.pieces_ref = f32[32,8,512]{2,1,0:T(8,128)S(1)} all-to-all(f32[32,8,512]{2,1,0:T(8,128)S(1)} %bitcast.1), channel_id=1, replica_groups=mesh['row'=32,'col'=8] {'row'}, dimensions={0} | all-to-all | bytes 1048576 | tf_op jit(solution)/shard_map/all_to_all | solution.py:382
  53.1 1.1 scan.1
  54.2 4.9 %all-to-all-start.1 = ((f32[32,16,512]{2,1,0:T(8,128)}), f32[32,16,512]{2,1,0:T(8,128)S(1)}, u32[]{:S(2)}, u32[]{:S(2)}) async-start(f32[32,16,512]{2,1,0:T(8,128)} %scan.1), calls=%async_computation.1 | async-start | bytes 2097152 | tf_op jit(solution)/shard_map/all_to_all | solution.py:382
  59.1 2.8 %collective-permute-start.9 = (f32[32,256]{1,0:T(8,128)S(1)}, f32[32,256]{1,0:T(8,128)S(1)}, u32[]{:S(2)}, u32[]{:S(2)}) collective-permute-start(f32[32,256]{1,0:T(8,128)S(1)} %get-tuple-element.25.own_ref), channel_id=1, source_target_pairs={{0,16},{8,24},{16,0},{24,8},{32,48},{40,56},{48,32},{56,40},{64,80... | collective-permute-start | bytes 98312 | tf_op jit(solution)/shard_map/ppermute | solution.py:45
  64.3 2.4 %collective-permute-done.8.three_ref = f32[32,256]{1,0:T(8,128)S(1)} collective-permute-done((f32[32,256]{1,0:T(8,128)S(1)}, f32[32,256]{1,0:T(8,128)S(1)}, u32[]{:S(2)}, u32[]{:S(2)}) %collective-permute-start.8) | collective-permute-done | bytes 32800 | tf_op jit(solution)/shard_map/ppermute | solution.py:45
  66.7 1.3 %collective-permute-done.7.one_ref = f32[32,256]{1,0:T(8,128)S(1)} collective-permute-done((f32[32,256]{1,0:T(8,128)S(1)}, f32[32,256]{1,0:T(8,128)S(1)}, u32[]{:S(2)}, u32[]{:S(2)}) %collective-permute-start.7) | collective-permute-done | bytes 32800 | tf_op jit(solution)/shard_map/ppermute | solution.py:45
  68.1 1.3 collective-permute-start.10
  69.4 13.4 %collective-permute-done.10.other_ref = f32[32,256]{1,0:T(8,128)S(1)} collective-permute-done((f32[32,256]{1,0:T(8,128)S(1)}, f32[32,256]{1,0:T(8,128)S(1)}, u32[]{:S(2)}, u32[]{:S(2)}) %collective-permute-start.10) | collective-permute-done | bytes 32800 | tf_op jit(solution)/shard_map/ppermute | solution.py:45
  82.8 3.2 %collective-permute-start.13 = (f32[32,256]{1,0:T(8,128)S(1)}, f32[32,256]{1,0:T(8,128)S(1)}, u32[]{:S(2)}, u32[]{:S(2)}) collective-permute-start(f32[32,256]{1,0:T(8,128)S(1)} %get-tuple-element.29.own_ref), channel_id=1, source_target_pairs={{0,128},{8,136},{16,144},{24,152},{32,160},{40,168},{48,176},{56,1... | collective-permute-start | bytes 98312 | tf_op jit(solution)/shard_map/ppermute | solution.py:45
  86.0 1.1 collective-permute-start.12
  87.1 1.3 collective-permute-start.11
  88.4 1.2 collective-permute-done.13.two_ref
  89.7 3.1 %collective-permute-done.11.one_ref = f32[32,256]{1,0:T(8,128)S(1)} collective-permute-done((f32[32,256]{1,0:T(8,128)S(1)}, f32[32,256]{1,0:T(8,128)S(1)}, u32[]{:S(2)}, u32[]{:S(2)}) %collective-permute-start.11) | collective-permute-done | bytes 32800 | tf_op jit(solution)/shard_map/ppermute | solution.py:45
  92.9 2.2 %collective-permute-start.16 = (f32[2,32,256]{2,1,0:T(8,128)S(1)}, f32[2,32,256]{2,1,0:T(8,128)S(1)}, u32[]{:S(2)}, u32[]{:S(2)}) collective-permute-start(f32[2,32,256]{2,1,0:T(8,128)S(1)} %shard_map.51.refs_0_), channel_id=1, source_target_pairs={{0,4},{1,5},{2,6},{3,7},{4,0},{5,1},{6,2},{7,3},{8,12},{9,13},{10,... | collective-permute-start | bytes 196616 | tf_op jit(solution)/shard_map/ppermute | solution.py:45
  95.1 1.2 collective-permute-start.15
  96.6 4.6 %collective-permute-start.17 = (f32[2,32,256]{2,1,0:T(8,128)S(1)}, f32[2,32,256]{2,1,0:T(8,128)S(1)}, u32[]{:S(2)}, u32[]{:S(2)}) collective-permute-start(f32[2,32,256]{2,1,0:T(8,128)S(1)} %shard_map.51.refs_0_), channel_id=1, source_target_pairs={{0,1},{1,0},{2,3},{3,2},{4,5},{5,4},{6,7},{7,6},{8,9},{9,8},{10,11... | collective-permute-start | bytes 196616 | tf_op jit(solution)/shard_map/ppermute | solution.py:45
  101.2 1.3 collective-permute-start.20
  102.5 0.9 collective-permute-start.19
  103.4 2.6 %collective-permute-start.18 = (f32[2,32,256]{2,1,0:T(8,128)S(1)}, f32[2,32,256]{2,1,0:T(8,128)S(1)}, u32[]{:S(2)}, u32[]{:S(2)}) collective-permute-start(f32[2,32,256]{2,1,0:T(8,128)S(1)} %collective-permute-done.14.refs_1_), channel_id=1, source_target_pairs={{0,1},{1,0},{2,3},{3,2},{4,5},{5,4},{6,7},{7,6},{8,9},{9,8},{10,11... | collective-permute-start | bytes 196616 | tf_op jit(solution)/shard_map/ppermute | solution.py:45
  106.0 2.2 %turn.1 = (bf16[2048,256]{1,0:T(8,128)(2,1)}, bf16[2048,256]{1,0:T(8,128)(2,1)}) custom-call(bf16[256,2048]{1,0:T(8,128)(2,1)S(1)} %get-tuple-element.30.high_ref, bf16[256,2048]{1,0:T(8,128)(2,1)S(1)} %get-tuple-element.31.low_ref), custom_call_target="tpu_custom_call" | custom-call | flops 1500000000 | bytes 3000000 | tf_op jit(solution)/shard_map/turn/pallas_call | solution.py:119
  108.3 14.7 %factor.1 = (f32[256,256]{1,0:T(8,128)}, bf16[2,256,256]{2,1,0:T(8,128)(2,1)}, bf16[2,256,256]{2,1,0:T(8,128)(2,1)}) custom-call(f32[2,32,256]{2,1,0:T(8,128)S(1)} %shard_map.51.refs_0_, f32[2,32,256]{2,1,0:T(8,128)S(1)} %collective-permute-done.14.refs_1_, f32[2,32,256]{2,1,0:T(8,128)S(1)} %collective-permute-done.15.refs_2_, ...), custom_call_target="tpu_custom_call" | custom-call | flops 8000000000 | bytes 16000000 | tf_op jit(solution)/shard_map/factor/pallas_call | solution.py:309
  123.0 9.2 %project.1 = (f32[256,512]{1,0:T(8,128)}, f32[2048,512]{1,0:T(8,128)}) custom-call(bf16[2,256,256]{2,1,0:T(8,128)(2,1)} %get-tuple-element.41.sh_ref, bf16[2,256,256]{2,1,0:T(8,128)(2,1)} %get-tuple-element.42.sl_ref, f32[32,16,512]{2,1,0:T(8,128)S(1)} %all-to-all-done.1.sums_ref, bf16[2048,256]{1,0:T(8,128)(2,1)} %get-tuple-element.43.high_ref, ...), custom_call_target="tpu_custom_call" | custom-call | flops 4000000000 | bytes 8000000 | tf_op jit(solution)/shard_map/project/pallas_call | solution.py:348
  (26 shorter events, 4.7 us)
Async XLA Ops:
  0.6 22.4 %copy-start = (f32[2048,512]{1,0:T(8,128)S(1)}, f32[2048,512]{1,0:T(8,128)}, u32[]{:S(2)}) copy-start(f32[2048,512]{1,0:T(8,128)} %trailing_ref.3) | copy-start | bytes 12582916
  0.6 9.2 %collective-permute-start.2 = (f32[32,2048]{1,0:T(8,128)}, f32[32,2048]{1,0:T(8,128)S(1)}, u32[]{:S(2)}, u32[]{:S(2)}) collective-permute-start(f32[32,2048]{1,0:T(8,128)} %refs_0_.1), channel_id=1, source_target_pairs={{0,4},{1,5},{2,6},{3,7},{4,0},{5,1},{6,2},{7,3},{8,12},{9,13},{10,... | collective-permute-start | bytes 786440 | tf_op jit(solution)/shard_map/ppermute | solution.py:45
  4.5 12.1 %collective-permute-start.1 = (f32[32,2048]{1,0:T(8,128)}, f32[32,2048]{1,0:T(8,128)S(1)}, u32[]{:S(2)}, u32[]{:S(2)}) collective-permute-start(f32[32,2048]{1,0:T(8,128)} %refs_0_.1), channel_id=1, source_target_pairs={{0,6},{1,7},{2,0},{3,1},{4,2},{5,3},{6,4},{7,5},{8,14},{9,15},{10,... | collective-permute-start | bytes 786440 | tf_op jit(solution)/shard_map/ppermute | solution.py:45
  5.2 12.8 %collective-permute-start = (f32[32,2048]{1,0:T(8,128)}, f32[32,2048]{1,0:T(8,128)S(1)}, u32[]{:S(2)}, u32[]{:S(2)}) collective-permute-start(f32[32,2048]{1,0:T(8,128)} %refs_0_.1), channel_id=1, source_target_pairs={{0,2},{1,3},{2,4},{3,5},{4,6},{5,7},{6,0},{7,1},{8,10},{9,11},{10,... | collective-permute-start | bytes 786440 | tf_op jit(solution)/shard_map/ppermute | solution.py:45
  5.9 12.1 %collective-permute-start.3 = (f32[32,2048]{1,0:T(8,128)}, f32[32,2048]{1,0:T(8,128)S(1)}, u32[]{:S(2)}, u32[]{:S(2)}) collective-permute-start(f32[32,2048]{1,0:T(8,128)} %refs_0_.1), channel_id=1, source_target_pairs={{0,1},{1,0},{2,3},{3,2},{4,5},{5,4},{6,7},{7,6},{8,9},{9,8},{10,11... | collective-permute-start | bytes 786440 | tf_op jit(solution)/shard_map/ppermute | solution.py:45
  9.8 8.2 %collective-permute-start.6 = (f32[32,2048]{1,0:T(8,128)S(1)}, f32[32,2048]{1,0:T(8,128)S(1)}, u32[]{:S(2)}, u32[]{:S(2)}) collective-permute-start(f32[32,2048]{1,0:T(8,128)S(1)} %collective-permute-done.2.refs_3_), channel_id=1, source_target_pairs={{0,1},{1,0},{2,3},{3,2},{4,5},{5,4},{6,7},{7,6},{8,9},{9,8},{10,11... | collective-permute-start | bytes 786440 | tf_op jit(solution)/shard_map/ppermute | solution.py:45
  16.5 2.6 %collective-permute-start.5 = (f32[32,2048]{1,0:T(8,128)S(1)}, f32[32,2048]{1,0:T(8,128)S(1)}, u32[]{:S(2)}, u32[]{:S(2)}) collective-permute-start(f32[32,2048]{1,0:T(8,128)S(1)} %collective-permute-done.1.refs_2_), channel_id=1, source_target_pairs={{0,1},{1,0},{2,3},{3,2},{4,5},{5,4},{6,7},{7,6},{8,9},{9,8},{10,11... | collective-permute-start | bytes 786440 | tf_op jit(solution)/shard_map/ppermute | solution.py:45
  18.0 1.5 %collective-permute-start.4 = (f32[32,2048]{1,0:T(8,128)S(1)}, f32[32,2048]{1,0:T(8,128)S(1)}, u32[]{:S(2)}, u32[]{:S(2)}) collective-permute-start(f32[32,2048]{1,0:T(8,128)S(1)} %collective-permute-done.refs_1_), channel_id=1, source_target_pairs={{0,1},{1,0},{2,3},{3,2},{4,5},{5,4},{6,7},{7,6},{8,9},{9,8},{10,11... | collective-permute-start | bytes 786440 | tf_op jit(solution)/shard_map/ppermute | solution.py:45
  19.5 1.0 copy-start.1
  54.2 68.8 %all-to-all-start.1 = ((f32[32,16,512]{2,1,0:T(8,128)}), f32[32,16,512]{2,1,0:T(8,128)S(1)}, u32[]{:S(2)}, u32[]{:S(2)}) async-start(f32[32,16,512]{2,1,0:T(8,128)} %scan.1), calls=%async_computation.1 | async-start | bytes 2097152 | tf_op jit(solution)/shard_map/all_to_all | solution.py:382
  59.1 5.2 %collective-permute-start.9 = (f32[32,256]{1,0:T(8,128)S(1)}, f32[32,256]{1,0:T(8,128)S(1)}, u32[]{:S(2)}, u32[]{:S(2)}) collective-permute-start(f32[32,256]{1,0:T(8,128)S(1)} %get-tuple-element.25.own_ref), channel_id=1, source_target_pairs={{0,16},{8,24},{16,0},{24,8},{32,48},{40,56},{48,32},{56,40},{64,80... | collective-permute-start | bytes 98312 | tf_op jit(solution)/shard_map/ppermute | solution.py:45
  61.9 4.8 %collective-permute-start.8 = (f32[32,256]{1,0:T(8,128)S(1)}, f32[32,256]{1,0:T(8,128)S(1)}, u32[]{:S(2)}, u32[]{:S(2)}) collective-permute-start(f32[32,256]{1,0:T(8,128)S(1)} %get-tuple-element.25.own_ref), channel_id=1, source_target_pairs={{0,24},{8,0},{16,8},{24,16},{32,56},{40,32},{48,40},{56,48},{64,88... | collective-permute-start | bytes 98312 | tf_op jit(solution)/shard_map/ppermute | solution.py:45
  62.8 5.2 %collective-permute-start.7 = (f32[32,256]{1,0:T(8,128)S(1)}, f32[32,256]{1,0:T(8,128)S(1)}, u32[]{:S(2)}, u32[]{:S(2)}) collective-permute-start(f32[32,256]{1,0:T(8,128)S(1)} %get-tuple-element.25.own_ref), channel_id=1, source_target_pairs={{0,8},{8,16},{16,24},{24,0},{32,40},{40,48},{48,56},{56,32},{64,72... | collective-permute-start | bytes 98312 | tf_op jit(solution)/shard_map/ppermute | solution.py:45
  68.1 14.7 %collective-permute-start.10 = (f32[32,256]{1,0:T(8,128)S(1)}, f32[32,256]{1,0:T(8,128)S(1)}, u32[]{:S(2)}, u32[]{:S(2)}) collective-permute-start(f32[32,256]{1,0:T(8,128)S(1)} %get-tuple-element.27.total_ref), channel_id=1, source_target_pairs={{0,32},{8,40},{16,48},{24,56},{32,0},{40,8},{48,16},{56,24},{64,96... | collective-permute-start | bytes 98312 | tf_op jit(solution)/shard_map/ppermute | solution.py:45
  82.8 6.8 %collective-permute-start.13 = (f32[32,256]{1,0:T(8,128)S(1)}, f32[32,256]{1,0:T(8,128)S(1)}, u32[]{:S(2)}, u32[]{:S(2)}) collective-permute-start(f32[32,256]{1,0:T(8,128)S(1)} %get-tuple-element.29.own_ref), channel_id=1, source_target_pairs={{0,128},{8,136},{16,144},{24,152},{32,160},{40,168},{48,176},{56,1... | collective-permute-start | bytes 98312 | tf_op jit(solution)/shard_map/ppermute | solution.py:45
  86.0 3.7 %collective-permute-start.12 = (f32[32,256]{1,0:T(8,128)S(1)}, f32[32,256]{1,0:T(8,128)S(1)}, u32[]{:S(2)}, u32[]{:S(2)}) collective-permute-start(f32[32,256]{1,0:T(8,128)S(1)} %get-tuple-element.29.own_ref), channel_id=1, source_target_pairs={{0,192},{8,200},{16,208},{24,216},{32,224},{40,232},{48,240},{56,2... | collective-permute-start | bytes 98312 | tf_op jit(solution)/shard_map/ppermute | solution.py:45
  87.1 5.7 %collective-permute-start.11 = (f32[32,256]{1,0:T(8,128)S(1)}, f32[32,256]{1,0:T(8,128)S(1)}, u32[]{:S(2)}, u32[]{:S(2)}) collective-permute-start(f32[32,256]{1,0:T(8,128)S(1)} %get-tuple-element.29.own_ref), channel_id=1, source_target_pairs={{0,64},{8,72},{16,80},{24,88},{32,96},{40,104},{48,112},{56,120},{... | collective-permute-start | bytes 98312 | tf_op jit(solution)/shard_map/ppermute | solution.py:45
  92.9 8.3 %collective-permute-start.16 = (f32[2,32,256]{2,1,0:T(8,128)S(1)}, f32[2,32,256]{2,1,0:T(8,128)S(1)}, u32[]{:S(2)}, u32[]{:S(2)}) collective-permute-start(f32[2,32,256]{2,1,0:T(8,128)S(1)} %shard_map.51.refs_0_), channel_id=1, source_target_pairs={{0,4},{1,5},{2,6},{3,7},{4,0},{5,1},{6,2},{7,3},{8,12},{9,13},{10,... | collective-permute-start | bytes 196616 | tf_op jit(solution)/shard_map/ppermute | solution.py:45
  95.1 7.4 %collective-permute-start.15 = (f32[2,32,256]{2,1,0:T(8,128)S(1)}, f32[2,32,256]{2,1,0:T(8,128)S(1)}, u32[]{:S(2)}, u32[]{:S(2)}) collective-permute-start(f32[2,32,256]{2,1,0:T(8,128)S(1)} %shard_map.51.refs_0_), channel_id=1, source_target_pairs={{0,6},{1,7},{2,0},{3,1},{4,2},{5,3},{6,4},{7,5},{8,14},{9,15},{10,... | collective-permute-start | bytes 196616 | tf_op jit(solution)/shard_map/ppermute | solution.py:45
  96.3 7.1 %collective-permute-start.14 = (f32[2,32,256]{2,1,0:T(8,128)S(1)}, f32[2,32,256]{2,1,0:T(8,128)S(1)}, u32[]{:S(2)}, u32[]{:S(2)}) collective-permute-start(f32[2,32,256]{2,1,0:T(8,128)S(1)} %shard_map.51.refs_0_), channel_id=1, source_target_pairs={{0,2},{1,3},{2,4},{3,5},{4,6},{5,7},{6,0},{7,1},{8,10},{9,11},{10,... | collective-permute-start | bytes 196616 | tf_op jit(solution)/shard_map/ppermute | solution.py:45
  96.6 11.7 %collective-permute-start.17 = (f32[2,32,256]{2,1,0:T(8,128)S(1)}, f32[2,32,256]{2,1,0:T(8,128)S(1)}, u32[]{:S(2)}, u32[]{:S(2)}) collective-permute-start(f32[2,32,256]{2,1,0:T(8,128)S(1)} %shard_map.51.refs_0_), channel_id=1, source_target_pairs={{0,1},{1,0},{2,3},{3,2},{4,5},{5,4},{6,7},{7,6},{8,9},{9,8},{10,11... | collective-permute-start | bytes 196616 | tf_op jit(solution)/shard_map/ppermute | solution.py:45
  101.2 7.1 %collective-permute-start.20 = (f32[2,32,256]{2,1,0:T(8,128)S(1)}, f32[2,32,256]{2,1,0:T(8,128)S(1)}, u32[]{:S(2)}, u32[]{:S(2)}) collective-permute-start(f32[2,32,256]{2,1,0:T(8,128)S(1)} %collective-permute-done.16.refs_3_), channel_id=1, source_target_pairs={{0,1},{1,0},{2,3},{3,2},{4,5},{5,4},{6,7},{7,6},{8,9},{9,8},{10,11... | collective-permute-start | bytes 196616 | tf_op jit(solution)/shard_map/ppermute | solution.py:45
  102.5 5.8 %collective-permute-start.19 = (f32[2,32,256]{2,1,0:T(8,128)S(1)}, f32[2,32,256]{2,1,0:T(8,128)S(1)}, u32[]{:S(2)}, u32[]{:S(2)}) collective-permute-start(f32[2,32,256]{2,1,0:T(8,128)S(1)} %collective-permute-done.15.refs_2_), channel_id=1, source_target_pairs={{0,1},{1,0},{2,3},{3,2},{4,5},{5,4},{6,7},{7,6},{8,9},{9,8},{10,11... | collective-permute-start | bytes 196616 | tf_op jit(solution)/shard_map/ppermute | solution.py:45
  103.4 4.9 %collective-permute-start.18 = (f32[2,32,256]{2,1,0:T(8,128)S(1)}, f32[2,32,256]{2,1,0:T(8,128)S(1)}, u32[]{:S(2)}, u32[]{:S(2)}) collective-permute-start(f32[2,32,256]{2,1,0:T(8,128)S(1)} %collective-permute-done.14.refs_1_), channel_id=1, source_target_pairs={{0,1},{1,0},{2,3},{3,2},{4,5},{5,4},{6,7},{7,6},{8,9},{9,8},{10,11... | collective-permute-start | bytes 196616 | tf_op jit(solution)/shard_map/ppermute | solution.py:45
where the time goes:
time: 133 us; the launch traced here: 132 us
  starting transfers between devices  42.6 us (32%)
  Pallas kernels  32.4 us (24%)
  waiting for transfers between devices  28.1 us (21%)
  blocking collectives  27.5 us (21%)
    ppermute x21, starting transfers between devices, rotate(): return lax.ppermute(value, axis, pairs)  37.6 us
    ppermute x21, waiting for transfers between devices, rotate(): return lax.ppermute(value, axis, pairs)  28.1 us
    all_to_all x1, blocking collectives, exchange(): return lax.all_to_all(value, 'row', 0, 0, tiled=True)  27.5 us
    pallas_call x1, Pallas kernels, factor(): pl.pallas_call(factor_kernel, out_shape=[jax.ShapeDtypeStruct((order, ord...  14.7 us
    pallas_call x1, Pallas kernels, project(): pl.pallas_call(project_kernel, grid=(rows // block,), in_specs=[whole, wh...  9.17 us
    all_to_all x1, starting transfers between devices, exchange(): return lax.all_to_all(value, 'row', 0, 0, tiled=True)  4.93 us
  transfers between devices with their start and end apart: 22, of which 11 were waited for; matrix products, arithmetic and copies ran while one was open for 0% of the time, Pallas kernels for 13%

commit v1 on v0

--- a/solution.py
+++ b/solution.py
@@ -41,6 +41,10 @@
     return pl.CostEstimate(flops=int(us * 5e8), bytes_accessed=int(us * 1e6), transcendentals=0)
 
 
+def in_hbm(value):
+    return pltpu.with_memory_space_constraint(value, pltpu.HBM)
+
+
 def rotate(value, axis, pairs):
     return lax.ppermute(value, axis, pairs)
 
@@ -80,17 +84,25 @@
     return [rotate(value, "row", [(i, (i + 2 * X * k) % count) for i in range(count)]) for k in (1, 3, 2)]
 
 
-def gather_kernel(*refs):
-    pieces, (high_ref, low_ref, gram_ref, whole_ref) = refs[:-4], refs[-4:]
-    height = pieces[0].shape[0]
-    for piece, owner in zip(pieces, chip_offsets()):
+def gather_kernel(panel_ref, *refs):
+    pieces, (high_ref, low_ref, gram_ref, whole_ref, own_ref, arrived) = refs[:-6], refs[-6:]
+    height = own_ref.shape[0]
+    fetch = pltpu.make_async_copy(panel_ref, own_ref, arrived)
+    fetch.start()
+    owners = chip_offsets()
+
+    def place(value, owner):
         rows = pl.ds(pl.multiple_of(owner * height, height), height)
-        value = piece[...]
         whole_ref[rows, :] = value
         high, low = halves(value)
         high_ref[rows, :] = high
         low_ref[rows, :] = low
-    gram_ref[...] = dot(pieces[0][...], whole_ref[...], (1, 1))
+
+    for piece, owner in zip(pieces, owners[1:]):
+        place(piece[...], owner)
+    fetch.wait()
+    place(own_ref[...], owners[0])
+    gram_ref[...] = dot(own_ref[...], whole_ref[...], (1, 1))
 
 
 def gather(pieces):
@@ -99,12 +111,13 @@
     shapes = [(width, rows, BF16), (width, rows, BF16), (height, width, F32)]
     return pl.pallas_call(
         gather_kernel,
+        in_specs=[pl.BlockSpec(memory_space=pl.ANY)] + [pl.BlockSpec(memory_space=pltpu.VMEM)] * (len(pieces) - 1),
         out_shape=[jax.ShapeDtypeStruct((a, b), t) for a, b, t in shapes],
-        scratch_shapes=[pltpu.VMEM((width, rows), F32)],
+        scratch_shapes=[pltpu.VMEM((width, rows), F32), pltpu.VMEM((height, rows), F32), pltpu.SemaphoreType.DMA],
         cost_estimate=cost(4),
         compiler_params=room(16),
         name="gather",
-    )(*pieces)
+    )(in_hbm(pieces[0]), *pieces[1:])
 
 
 def turn_kernel(high_ref, low_ref, high_out, low_out):
@@ -128,32 +141,55 @@
     )(high, low)
 
 
-def cross_kernel(high_ref, low_ref, trailing_ref, out_ref):
+def halve_kernel(value_ref, high_ref, low_ref):
+    high_ref[...], low_ref[...] = halves(value_ref[...])
+
+
+def halve(value):
+    rows, columns = value.shape
+    block = 256
+    spec = pl.BlockSpec((block, columns), lambda i: (i, 0))
+    shape = jax.ShapeDtypeStruct(value.shape, BF16)
+    return pl.pallas_call(
+        halve_kernel,
+        grid=(rows // block,),
+        in_specs=[spec],
+        out_specs=[spec] * 2,
+        out_shape=[shape] * 2,
+        cost_estimate=cost(2),
+        compiler_params=room(8),
+        name="halve",
+    )(in_hbm(value))
+
+
+def cross_kernel(high_ref, low_ref, right_high_ref, right_low_ref, out_ref):
+    product = dot3((high_ref[...], low_ref[...]), (right_high_ref[...], right_low_ref[...]))
+
     @pl.when(pl.program_id(0) == 0)
     def _():
-        out_ref[...] = jnp.zeros_like(out_ref)
-
-    out_ref[...] += dot3((high_ref[...], low_ref[...]), halves(trailing_ref[...]))
-
-
-def cross(high, low, trailing):
+        out_ref[...] = product
+
+    @pl.when(pl.program_id(0) > 0)
+    def _():
+        out_ref[...] += product
+
+
+def cross(high, low, right_high, right_low):
     width, rows = high.shape
-    columns = trailing.shape[1]
-    block = 512
+    columns = right_high.shape[1]
+    block = 1024
+    left = pl.BlockSpec((width, block), lambda i: (0, i))
+    right = pl.BlockSpec((block, columns), lambda i: (i, 0))
     return pl.pallas_call(
         cross_kernel,
         grid=(rows // block,),
-        in_specs=[
-            pl.BlockSpec((width, block), lambda i: (0, i)),
-            pl.BlockSpec((width, block), lambda i: (0, i)),
-            pl.BlockSpec((block, columns), lambda i: (i, 0)),
-        ],
+        in_specs=[left, left, right, right],
         out_specs=pl.BlockSpec((width, columns), lambda i: (0, 0)),
         out_shape=jax.ShapeDtypeStruct((width, columns), F32),
-        cost_estimate=cost(5),
+        cost_estimate=cost(4),
         compiler_params=room(16),
         name="cross",
-    )(high, low, trailing)
+    )(high, low, right_high, right_low)
 
 
 def group_kernel(own_ref, one_ref, three_ref, two_ref, prefix_ref, total_ref):
@@ -320,55 +356,75 @@
     )(*pieces)
 
 
-def project_kernel(sh_ref, sl_ref, sums_ref, high_ref, low_ref, trailing_ref, blocks_ref, out_ref, ch_ref, cl_ref):
+def project_kernel(sums_ref, *refs):
+    (sh_from, sl_from, high_from, low_from, trailing_from, blocks_to, out_to), refs = refs[:7], refs[7:]
+    sh_ref, sl_ref, high_ref, low_ref, trailing_ref, blocks_ref, out_ref, first, coming, going = refs
     stops, both, columns = sums_ref.shape
     height = both // 2
-
-    @pl.when(pl.program_id(0) == 0)
-    def _():
-        total = sums_ref[:, height:, :].reshape(stops * height, columns)
-        high, low = halves(dot3((sh_ref[1], sl_ref[1]), halves(total)))
-        ch_ref[...] = high
-        cl_ref[...] = low
-        prefix = sums_ref[:, :height, :].reshape(stops * height, columns)
-        blocks_ref[...] = dot3((sh_ref[0], sl_ref[0]), halves(prefix))
-
-    out_ref[...] = trailing_ref[...] - dot3((high_ref[...], low_ref[...]), (ch_ref[...], cl_ref[...]))
-
-
-def in_hbm(value):
-    return pltpu.with_memory_space_constraint(value, pltpu.HBM)
+    rows = trailing_ref.shape[0]
+    chunks = coming.shape[0]
+    size = rows // chunks
+    solves = [
+        pltpu.make_async_copy(sh_from, sh_ref, first.at[0]),
+        pltpu.make_async_copy(sl_from, sl_ref, first.at[1]),
+    ]
+    for copy in solves:
+        copy.start()
+    arrivals = []
+    for i in range(chunks):
+        part = pl.ds(i * size, size)
+        arrivals.append(
+            [
+                pltpu.make_async_copy(source.at[part], target.at[part], coming.at[i, k])
+                for k, (source, target) in enumerate(
+                    ((high_from, high_ref), (low_from, low_ref), (trailing_from, trailing_ref))
+                )
+            ]
+        )
+        for copy in arrivals[-1]:
+            copy.start()
+    total = halves(sums_ref[:, height:, :].reshape(stops * height, columns))
+    prefix = halves(sums_ref[:, :height, :].reshape(stops * height, columns))
+    for copy in solves:
+        copy.wait()
+    coeffs = halves(dot3((sh_ref[1], sl_ref[1]), total))
+    blocks_ref[...] = dot3((sh_ref[0], sl_ref[0]), prefix)
+    leaving = [pltpu.make_async_copy(blocks_ref, blocks_to, going.at[chunks])]
+    leaving[0].start()
+    for i in range(chunks):
+        part = pl.ds(i * size, size)
+        for copy in arrivals[i]:
+            copy.wait()
+        out_ref[part, :] = trailing_ref[part, :] - dot3((high_ref[part, :], low_ref[part, :]), coeffs)
+        leaving.append(pltpu.make_async_copy(out_ref.at[part], out_to.at[part], going.at[i]))
+        leaving[-1].start()
+    for copy in leaving:
+        copy.wait()
 
 
 def project(solves, sums, high, low, trailing):
     rows, columns = trailing.shape
     width = high.shape[1]
-    block = 256
-    whole = pl.BlockSpec(solves[0].shape, lambda i: (0, 0, 0))
+    chunks = 8
+    anywhere = pl.BlockSpec(memory_space=pl.ANY)
     return pl.pallas_call(
         project_kernel,
-        grid=(rows // block,),
-        in_specs=[
-            whole,
-            whole,
-            pl.BlockSpec(sums.shape, lambda i: (0, 0, 0)),
-            pl.BlockSpec((block, width), lambda i: (i, 0)),
-            pl.BlockSpec((block, width), lambda i: (i, 0)),
-            pl.BlockSpec((block, columns), lambda i: (i, 0)),
+        in_specs=[pl.BlockSpec(memory_space=pltpu.VMEM)] + [anywhere] * 5,
+        out_specs=[anywhere] * 2,
+        out_shape=[pltpu.HBM((width, columns), F32), pltpu.HBM((rows, columns), F32)],
+        scratch_shapes=[pltpu.VMEM(s.shape, BF16) for s in (*solves, high, low)]
+        + [
+            pltpu.VMEM((rows, columns), F32),
+            pltpu.VMEM((width, columns), F32),
+            pltpu.VMEM((rows, columns), F32),
+            pltpu.SemaphoreType.DMA((2,)),
+            pltpu.SemaphoreType.DMA((chunks, 3)),
+            pltpu.SemaphoreType.DMA((chunks + 1,)),
         ],
-        out_specs=[
-            pl.BlockSpec((width, columns), lambda i: (0, 0)),
-            pl.BlockSpec((block, columns), lambda i: (i, 0)),
-        ],
-        out_shape=[
-            jax.ShapeDtypeStruct((width, columns), F32),
-            jax.ShapeDtypeStruct((rows, columns), F32),
-        ],
-        scratch_shapes=[pltpu.VMEM((width, columns), BF16)] * 2,
-        cost_estimate=cost(8),
-        compiler_params=room(16),
+        cost_estimate=cost(6),
+        compiler_params=room(24),
         name="project",
-    )(*[in_hbm(s) for s in solves], sums, in_hbm(high), in_hbm(low), in_hbm(trailing))
+    )(sums, *[in_hbm(v) for v in (*solves, high, low, trailing)])
 
 
 def stages(panel_transposed, trailing):
@@ -382,7 +438,7 @@
         return lax.all_to_all(value, "row", 0, 0, tiled=True)
 
     behind = from_stops_x(own_gram)
-    own_cross = cross(high, low, trailing)
+    own_cross = cross(high, low, *halve(trailing))
     pieces = exchange(own_cross.reshape(stops, width // stops, columns))
 
     prefix, total = small(group_kernel, [piece] * 2, own_gram, *behind)

time: 133 us -> 135 us (1.015)
  waiting for transfers between devices: 28.1 us -> 21.2 us
  starting transfers between devices: 42.6 us -> 49 us
  Pallas kernels: 32.4 us -> 35.8 us
    ppermute x21, waiting for transfers between devices: 28.1 us -> 21.2 us  [rotate(): return lax.ppermute(value, axis, pairs)]
    ppermute x21, starting transfers between devices: 37.6 us -> 43.9 us  [rotate(): return lax.ppermute(value, axis, pairs)]
    pallas_call x3 -> x4, Pallas kernels: 14.3 us -> 17.8 us  [the longest x1 7.5 us: project(): pl.pallas_call(project_kernel, in_specs=[pl.BlockSpec(memory_space=pltpu....]
  transfers between devices with their start and end apart: 22 -> 22, of which waited for: 11 -> 4; matrix products, arithmetic and copies ran while one was open for 0% -> 0% of each run, Pallas kernels for 13% -> 16%
where the time goes in v1:
time: 135 us; the launch traced here: 134 us
  starting transfers between devices  49 us (36%)
  Pallas kernels  35.8 us (27%)
  blocking collectives  27.6 us (20%)
  waiting for transfers between devices  21.2 us (16%)
    ppermute x21, starting transfers between devices, rotate(): return lax.ppermute(value, axis, pairs)  43.9 us
    all_to_all x1, blocking collectives, exchange(): return lax.all_to_all(value, 'row', 0, 0, tiled=True)  27.6 us
    ppermute x21, waiting for transfers between devices, rotate(): return lax.ppermute(value, axis, pairs)  21.2 us
    pallas_call x1, Pallas kernels, factor(): pl.pallas_call(factor_kernel, out_shape=[jax.ShapeDtypeStruct((order, ord...  14.7 us
    pallas_call x1, Pallas kernels, project(): pl.pallas_call(project_kernel, in_specs=[pl.BlockSpec(memory_space=pltpu....  7.5 us
    all_to_all x1, starting transfers between devices, exchange(): return lax.all_to_all(value, 'row', 0, 0, tiled=True)  5.05 us
    pallas_call x1, Pallas kernels, halve(): pl.pallas_call(halve_kernel, grid=(rows // block,), in_specs=[spec], out_...  4.83 us
    pallas_call x1, Pallas kernels, gather(): pl.pallas_call(gather_kernel, in_specs=[pl.BlockSpec(memory_space=pl.ANY)...  3.24 us
  transfers between devices with their start and end apart: 22, of which 4 were waited for; matrix products, arithmetic and copies ran while one was open for 0% of the time, Pallas kernels for 16%

profile of v1, /device:TPU:1, one launch (start us, length us, event | category | flops | bytes accessed | tf_op | source)
XLA Modules:
  0.0 134.5 jit_solution(14530073261820192188)
XLA Ops:
  0.6 2.2 %collective-permute-start = (f32[32,2048]{1,0:T(8,128)}, f32[32,2048]{1,0:T(8,128)S(1)}, u32[]{:S(2)}, u32[]{:S(2)}) collective-permute-start(f32[32,2048]{1,0:T(8,128)} %panel_ref.1), channel_id=1, source_target_pairs={{0,2},{1,3},{2,4},{3,5},{4,6},{5,7},{6,0},{7,1},{8,10},{9,11},{10,... | collective-permute-start | bytes 786440 | tf_op jit(solution)/shard_map/ppermute | solution.py:49
  2.8 1.5 %collective-permute-start.1 = (f32[32,2048]{1,0:T(8,128)}, f32[32,2048]{1,0:T(8,128)S(1)}, u32[]{:S(2)}, u32[]{:S(2)}) collective-permute-start(f32[32,2048]{1,0:T(8,128)} %panel_ref.1), channel_id=1, source_target_pairs={{0,6},{1,7},{2,0},{3,1},{4,2},{5,3},{6,4},{7,5},{8,14},{9,15},{10,... | collective-permute-start | bytes 786440 | tf_op jit(solution)/shard_map/ppermute | solution.py:49
  4.4 1.6 %collective-permute-start.2 = (f32[32,2048]{1,0:T(8,128)}, f32[32,2048]{1,0:T(8,128)S(1)}, u32[]{:S(2)}, u32[]{:S(2)}) collective-permute-start(f32[32,2048]{1,0:T(8,128)} %panel_ref.1), channel_id=1, source_target_pairs={{0,4},{1,5},{2,6},{3,7},{4,0},{5,1},{6,2},{7,3},{8,12},{9,13},{10,... | collective-permute-start | bytes 786440 | tf_op jit(solution)/shard_map/ppermute | solution.py:49
  5.9 1.5 %collective-permute-start.3 = (f32[32,2048]{1,0:T(8,128)}, f32[32,2048]{1,0:T(8,128)S(1)}, u32[]{:S(2)}, u32[]{:S(2)}) collective-permute-start(f32[32,2048]{1,0:T(8,128)} %panel_ref.1), channel_id=1, source_target_pairs={{0,1},{1,0},{2,3},{3,2},{4,5},{5,4},{6,7},{7,6},{8,9},{9,8},{10,11... | collective-permute-start | bytes 786440 | tf_op jit(solution)/shard_map/ppermute | solution.py:49
  7.4 1.1 collective-permute-done.refs_0_
  8.6 3.2 %collective-permute-start.4 = (f32[32,2048]{1,0:T(8,128)S(1)}, f32[32,2048]{1,0:T(8,128)S(1)}, u32[]{:S(2)}, u32[]{:S(2)}) collective-permute-start(f32[32,2048]{1,0:T(8,128)S(1)} %collective-permute-done.refs_0_), channel_id=1, source_target_pairs={{0,1},{1,0},{2,3},{3,2},{4,5},{5,4},{6,7},{7,6},{8,9},{9,8},{10,11... | collective-permute-start | bytes 786440 | tf_op jit(solution)/shard_map/ppermute | solution.py:49
  11.7 5.3 %collective-permute-start.5 = (f32[32,2048]{1,0:T(8,128)S(1)}, f32[32,2048]{1,0:T(8,128)S(1)}, u32[]{:S(2)}, u32[]{:S(2)}) collective-permute-start(f32[32,2048]{1,0:T(8,128)S(1)} %collective-permute-done.1.refs_1_), channel_id=1, source_target_pairs={{0,1},{1,0},{2,3},{3,2},{4,5},{5,4},{6,7},{7,6},{8,9},{9,8},{10,11... | collective-permute-start | bytes 786440 | tf_op jit(solution)/shard_map/ppermute | solution.py:49
  17.0 1.5 %collective-permute-start.6 = (f32[32,2048]{1,0:T(8,128)S(1)}, f32[32,2048]{1,0:T(8,128)S(1)}, u32[]{:S(2)}, u32[]{:S(2)}) collective-permute-start(f32[32,2048]{1,0:T(8,128)S(1)} %collective-permute-done.2.refs_2_), channel_id=1, source_target_pairs={{0,1},{1,0},{2,3},{3,2},{4,5},{5,4},{6,7},{7,6},{8,9},{9,8},{10,11... | collective-permute-start | bytes 786440 | tf_op jit(solution)/shard_map/ppermute | solution.py:49
  18.5 4.8 %halve.1 = (bf16[2048,512]{1,0:T(8,128)(2,1)S(1)}, bf16[2048,512]{1,0:T(8,128)(2,1)S(1)}) custom-call(f32[2048,512]{1,0:T(8,128)} %refs_4_.1), custom_call_target="tpu_custom_call" | custom-call | flops 1000000000 | bytes 2000000 | tf_op jit(solution)/shard_map/halve/pallas_call | solution.py:153
  23.4 3.2 %gather.1 = (bf16[256,2048]{1,0:T(8,128)(2,1)S(1)}, bf16[256,2048]{1,0:T(8,128)(2,1)S(1)}, f32[32,256]{1,0:T(8,128)S(1)}) custom-call(f32[32,2048]{1,0:T(8,128)} %panel_ref.1, f32[32,2048]{1,0:T(8,128)S(1)} %collective-permute-done.refs_0_, f32[32,2048]{1,0:T(8,128)S(1)} %collective-permute-done.1.refs_1_, f32[32,2048]{1,0:T(8,128)S(1)} %collective-permute-done.2.refs_2_, ...), custom_call_target="tpu_custom_call" | custom-call | flops 2000000000 | bytes 4000000 | tf_op jit(solution)/shard_map/gather/pallas_call | solution.py:112
  26.7 2.2 %cross.1 = f32[256,512]{1,0:T(8,128)S(1)} custom-call(bf16[256,2048]{1,0:T(8,128)(2,1)S(1)} %get-tuple-element.32.high_ref, bf16[256,2048]{1,0:T(8,128)(2,1)S(1)} %get-tuple-element.33.low_ref, bf16[2048,512]{1,0:T(8,128)(2,1)S(1)} %get-tuple-element.34.right_high_ref, bf16[2048,512]{1,0:T(8,128)(2,1)S(1)} %get-tuple-element.35.right_low_ref), custom_call_target="tpu_custom_call" | custom-call | flops 2000000000 | bytes 4000000 | tf_op jit(solution)/shard_map/cross/pallas_call | solution.py:183
  28.9 27.6 %all_to_all.10.pieces_ref = f32[32,8,512]{2,1,0:T(8,128)S(1)} all-to-all(f32[32,8,512]{2,1,0:T(8,128)S(1)} %bitcast.1), channel_id=1, replica_groups=mesh['row'=32,'col'=8] {'row'}, dimensions={0} | all-to-all | bytes 1048576 | tf_op jit(solution)/shard_map/all_to_all | solution.py:438
  56.4 1.1 scan.1
  57.5 5.1 %all-to-all-start.1 = ((f32[32,16,512]{2,1,0:T(8,128)}), f32[32,16,512]{2,1,0:T(8,128)S(1)}, u32[]{:S(2)}, u32[]{:S(2)}) async-start(f32[32,16,512]{2,1,0:T(8,128)} %scan.1), calls=%async_computation.1 | async-start | bytes 2097152 | tf_op jit(solution)/shard_map/all_to_all | solution.py:438
  62.6 1.3 collective-permute-start.7
  63.9 1.4 %collective-permute-start.8 = (f32[32,256]{1,0:T(8,128)S(1)}, f32[32,256]{1,0:T(8,128)S(1)}, u32[]{:S(2)}, u32[]{:S(2)}) collective-permute-start(f32[32,256]{1,0:T(8,128)S(1)} %get-tuple-element.27.own_ref), channel_id=1, source_target_pairs={{0,24},{8,0},{16,8},{24,16},{32,56},{40,32},{48,40},{56,48},{64,88... | collective-permute-start | bytes 98312 | tf_op jit(solution)/shard_map/ppermute | solution.py:49
  65.3 1.5 %collective-permute-start.9 = (f32[32,256]{1,0:T(8,128)S(1)}, f32[32,256]{1,0:T(8,128)S(1)}, u32[]{:S(2)}, u32[]{:S(2)}) collective-permute-start(f32[32,256]{1,0:T(8,128)S(1)} %get-tuple-element.27.own_ref), channel_id=1, source_target_pairs={{0,16},{8,24},{16,0},{24,8},{32,48},{40,56},{48,32},{56,40},{64,80... | collective-permute-start | bytes 98312 | tf_op jit(solution)/shard_map/ppermute | solution.py:49
  66.8 3.6 %collective-permute-done.9.two_ref = f32[32,256]{1,0:T(8,128)S(1)} collective-permute-done((f32[32,256]{1,0:T(8,128)S(1)}, f32[32,256]{1,0:T(8,128)S(1)}, u32[]{:S(2)}, u32[]{:S(2)}) %collective-permute-start.9) | collective-permute-done | bytes 32800 | tf_op jit(solution)/shard_map/ppermute | solution.py:49
  70.5 2.3 %collective-permute-start.10 = (f32[32,256]{1,0:T(8,128)S(1)}, f32[32,256]{1,0:T(8,128)S(1)}, u32[]{:S(2)}, u32[]{:S(2)}) collective-permute-start(f32[32,256]{1,0:T(8,128)S(1)} %get-tuple-element.29.total_ref), channel_id=1, source_target_pairs={{0,32},{8,40},{16,48},{24,56},{32,0},{40,8},{48,16},{56,24},{64,96... | collective-permute-start | bytes 98312 | tf_op jit(solution)/shard_map/ppermute | solution.py:49
  72.8 13.5 %collective-permute-done.10.other_ref = f32[32,256]{1,0:T(8,128)S(1)} collective-permute-done((f32[32,256]{1,0:T(8,128)S(1)}, f32[32,256]{1,0:T(8,128)S(1)}, u32[]{:S(2)}, u32[]{:S(2)}) %collective-permute-start.10) | collective-permute-done | bytes 32800 | tf_op jit(solution)/shard_map/ppermute | solution.py:49
  86.3 1.3 collective-permute-start.11
  87.6 2.3 %collective-permute-start.12 = (f32[32,256]{1,0:T(8,128)S(1)}, f32[32,256]{1,0:T(8,128)S(1)}, u32[]{:S(2)}, u32[]{:S(2)}) collective-permute-start(f32[32,256]{1,0:T(8,128)S(1)} %get-tuple-element.31.own_ref), channel_id=1, source_target_pairs={{0,192},{8,200},{16,208},{24,216},{32,224},{40,232},{48,240},{56,2... | collective-permute-start | bytes 98312 | tf_op jit(solution)/shard_map/ppermute | solution.py:49
  89.9 3.7 %collective-permute-start.13 = (f32[32,256]{1,0:T(8,128)S(1)}, f32[32,256]{1,0:T(8,128)S(1)}, u32[]{:S(2)}, u32[]{:S(2)}) collective-permute-start(f32[32,256]{1,0:T(8,128)S(1)} %get-tuple-element.31.own_ref), channel_id=1, source_target_pairs={{0,128},{8,136},{16,144},{24,152},{32,160},{40,168},{48,176},{56,1... | collective-permute-start | bytes 98312 | tf_op jit(solution)/shard_map/ppermute | solution.py:49
  93.6 2.9 %collective-permute-done.13.two_ref = f32[32,256]{1,0:T(8,128)S(1)} collective-permute-done((f32[32,256]{1,0:T(8,128)S(1)}, f32[32,256]{1,0:T(8,128)S(1)}, u32[]{:S(2)}, u32[]{:S(2)}) %collective-permute-start.13) | collective-permute-done | bytes 32800 | tf_op jit(solution)/shard_map/ppermute | solution.py:49
  96.6 0.9 collective-permute-start.14
  97.6 1.8 %collective-permute-start.15 = (f32[2,32,256]{2,1,0:T(8,128)S(1)}, f32[2,32,256]{2,1,0:T(8,128)S(1)}, u32[]{:S(2)}, u32[]{:S(2)}) collective-permute-start(f32[2,32,256]{2,1,0:T(8,128)S(1)} %shard_map.51.refs_0_), channel_id=1, source_target_pairs={{0,6},{1,7},{2,0},{3,1},{4,2},{5,3},{6,4},{7,5},{8,14},{9,15},{10,... | collective-permute-start | bytes 196616 | tf_op jit(solution)/shard_map/ppermute | solution.py:49
  99.4 4.7 %collective-permute-start.17 = (f32[2,32,256]{2,1,0:T(8,128)S(1)}, f32[2,32,256]{2,1,0:T(8,128)S(1)}, u32[]{:S(2)}, u32[]{:S(2)}) collective-permute-start(f32[2,32,256]{2,1,0:T(8,128)S(1)} %shard_map.51.refs_0_), channel_id=1, source_target_pairs={{0,1},{1,0},{2,3},{3,2},{4,5},{5,4},{6,7},{7,6},{8,9},{9,8},{10,11... | collective-permute-start | bytes 196616 | tf_op jit(solution)/shard_map/ppermute | solution.py:49
  104.1 2.2 %collective-permute-start.18 = (f32[2,32,256]{2,1,0:T(8,128)S(1)}, f32[2,32,256]{2,1,0:T(8,128)S(1)}, u32[]{:S(2)}, u32[]{:S(2)}) collective-permute-start(f32[2,32,256]{2,1,0:T(8,128)S(1)} %collective-permute-done.14.refs_1_), channel_id=1, source_target_pairs={{0,1},{1,0},{2,3},{3,2},{4,5},{5,4},{6,7},{7,6},{8,9},{9,8},{10,11... | collective-permute-start | bytes 196616 | tf_op jit(solution)/shard_map/ppermute | solution.py:49
  106.3 3.5 %collective-permute-start.20 = (f32[2,32,256]{2,1,0:T(8,128)S(1)}, f32[2,32,256]{2,1,0:T(8,128)S(1)}, u32[]{:S(2)}, u32[]{:S(2)}) collective-permute-start(f32[2,32,256]{2,1,0:T(8,128)S(1)} %collective-permute-done.16.refs_3_), channel_id=1, source_target_pairs={{0,1},{1,0},{2,3},{3,2},{4,5},{5,4},{6,7},{7,6},{8,9},{9,8},{10,11... | collective-permute-start | bytes 196616 | tf_op jit(solution)/shard_map/ppermute | solution.py:49
  109.8 2.2 %turn.1 = (bf16[2048,256]{1,0:T(8,128)(2,1)}, bf16[2048,256]{1,0:T(8,128)(2,1)}) custom-call(bf16[256,2048]{1,0:T(8,128)(2,1)S(1)} %get-tuple-element.32.high_ref, bf16[256,2048]{1,0:T(8,128)(2,1)S(1)} %get-tuple-element.33.low_ref), custom_call_target="tpu_custom_call" | custom-call | flops 1500000000 | bytes 3000000 | tf_op jit(solution)/shard_map/turn/pallas_call | solution.py:132
  112.0 14.7 %factor.1 = (f32[256,256]{1,0:T(8,128)}, bf16[2,256,256]{2,1,0:T(8,128)(2,1)}, bf16[2,256,256]{2,1,0:T(8,128)(2,1)}) custom-call(f32[2,32,256]{2,1,0:T(8,128)S(1)} %shard_map.51.refs_0_, f32[2,32,256]{2,1,0:T(8,128)S(1)} %collective-permute-done.14.refs_1_, f32[2,32,256]{2,1,0:T(8,128)S(1)} %collective-permute-done.15.refs_2_, ...), custom_call_target="tpu_custom_call" | custom-call | flops 8000000000 | bytes 16000000 | tf_op jit(solution)/shard_map/factor/pallas_call | solution.py:345
  126.8 7.5 %project.1 = (f32[256,512]{1,0:T(8,128)}, f32[2048,512]{1,0:T(8,128)}) custom-call(f32[32,16,512]{2,1,0:T(8,128)S(1)} %all-to-all-done.1.sums_ref, bf16[2,256,256]{2,1,0:T(8,128)(2,1)} %get-tuple-element.45.refs_0_, bf16[2,256,256]{2,1,0:T(8,128)(2,1)} %get-tuple-element.46.refs_1_, bf16[2048,256]{1,0:T(8,128)(2,1)} %get-tuple-element.47.refs_2_, ...), custom_call_target="tpu_custom_call" | custom-call | flops 3000000000 | bytes 6000000 | tf_op jit(solution)/shard_map/project/pallas_call | solution.py:410
  (23 shorter events, 0.2 us)
Async XLA Ops:
  0.6 7.9 %collective-permute-start = (f32[32,2048]{1,0:T(8,128)}, f32[32,2048]{1,0:T(8,128)S(1)}, u32[]{:S(2)}, u32[]{:S(2)}) collective-permute-start(f32[32,2048]{1,0:T(8,128)} %panel_ref.1), channel_id=1, source_target_pairs={{0,2},{1,3},{2,4},{3,5},{4,6},{5,7},{6,0},{7,1},{8,10},{9,11},{10,... | collective-permute-start | bytes 786440 | tf_op jit(solution)/shard_map/ppermute | solution.py:49
  2.8 8.9 %collective-permute-start.1 = (f32[32,2048]{1,0:T(8,128)}, f32[32,2048]{1,0:T(8,128)S(1)}, u32[]{:S(2)}, u32[]{:S(2)}) collective-permute-start(f32[32,2048]{1,0:T(8,128)} %panel_ref.1), channel_id=1, source_target_pairs={{0,6},{1,7},{2,0},{3,1},{4,2},{5,3},{6,4},{7,5},{8,14},{9,15},{10,... | collective-permute-start | bytes 786440 | tf_op jit(solution)/shard_map/ppermute | solution.py:49
  4.4 12.7 %collective-permute-start.2 = (f32[32,2048]{1,0:T(8,128)}, f32[32,2048]{1,0:T(8,128)S(1)}, u32[]{:S(2)}, u32[]{:S(2)}) collective-permute-start(f32[32,2048]{1,0:T(8,128)} %panel_ref.1), channel_id=1, source_target_pairs={{0,4},{1,5},{2,6},{3,7},{4,0},{5,1},{6,2},{7,3},{8,12},{9,13},{10,... | collective-permute-start | bytes 786440 | tf_op jit(solution)/shard_map/ppermute | solution.py:49
  5.9 17.5 %collective-permute-start.3 = (f32[32,2048]{1,0:T(8,128)}, f32[32,2048]{1,0:T(8,128)S(1)}, u32[]{:S(2)}, u32[]{:S(2)}) collective-permute-start(f32[32,2048]{1,0:T(8,128)} %panel_ref.1), channel_id=1, source_target_pairs={{0,1},{1,0},{2,3},{3,2},{4,5},{5,4},{6,7},{7,6},{8,9},{9,8},{10,11... | collective-permute-start | bytes 786440 | tf_op jit(solution)/shard_map/ppermute | solution.py:49
  8.6 14.8 %collective-permute-start.4 = (f32[32,2048]{1,0:T(8,128)S(1)}, f32[32,2048]{1,0:T(8,128)S(1)}, u32[]{:S(2)}, u32[]{:S(2)}) collective-permute-start(f32[32,2048]{1,0:T(8,128)S(1)} %collective-permute-done.refs_0_), channel_id=1, source_target_pairs={{0,1},{1,0},{2,3},{3,2},{4,5},{5,4},{6,7},{7,6},{8,9},{9,8},{10,11... | collective-permute-start | bytes 786440 | tf_op jit(solution)/shard_map/ppermute | solution.py:49
  11.7 11.7 %collective-permute-start.5 = (f32[32,2048]{1,0:T(8,128)S(1)}, f32[32,2048]{1,0:T(8,128)S(1)}, u32[]{:S(2)}, u32[]{:S(2)}) collective-permute-start(f32[32,2048]{1,0:T(8,128)S(1)} %collective-permute-done.1.refs_1_), channel_id=1, source_target_pairs={{0,1},{1,0},{2,3},{3,2},{4,5},{5,4},{6,7},{7,6},{8,9},{9,8},{10,11... | collective-permute-start | bytes 786440 | tf_op jit(solution)/shard_map/ppermute | solution.py:49
  17.0 6.4 %collective-permute-start.6 = (f32[32,2048]{1,0:T(8,128)S(1)}, f32[32,2048]{1,0:T(8,128)S(1)}, u32[]{:S(2)}, u32[]{:S(2)}) collective-permute-start(f32[32,2048]{1,0:T(8,128)S(1)} %collective-permute-done.2.refs_2_), channel_id=1, source_target_pairs={{0,1},{1,0},{2,3},{3,2},{4,5},{5,4},{6,7},{7,6},{8,9},{9,8},{10,11... | collective-permute-start | bytes 786440 | tf_op jit(solution)/shard_map/ppermute | solution.py:49
  57.5 69.3 %all-to-all-start.1 = ((f32[32,16,512]{2,1,0:T(8,128)}), f32[32,16,512]{2,1,0:T(8,128)S(1)}, u32[]{:S(2)}, u32[]{:S(2)}) async-start(f32[32,16,512]{2,1,0:T(8,128)} %scan.1), calls=%async_computation.1 | async-start | bytes 2097152 | tf_op jit(solution)/shard_map/all_to_all | solution.py:438
  62.6 4.3 %collective-permute-start.7 = (f32[32,256]{1,0:T(8,128)S(1)}, f32[32,256]{1,0:T(8,128)S(1)}, u32[]{:S(2)}, u32[]{:S(2)}) collective-permute-start(f32[32,256]{1,0:T(8,128)S(1)} %get-tuple-element.27.own_ref), channel_id=1, source_target_pairs={{0,8},{8,16},{16,24},{24,0},{32,40},{40,48},{48,56},{56,32},{64,72... | collective-permute-start | bytes 98312 | tf_op jit(solution)/shard_map/ppermute | solution.py:49
  63.9 3.0 %collective-permute-start.8 = (f32[32,256]{1,0:T(8,128)S(1)}, f32[32,256]{1,0:T(8,128)S(1)}, u32[]{:S(2)}, u32[]{:S(2)}) collective-permute-start(f32[32,256]{1,0:T(8,128)S(1)} %get-tuple-element.27.own_ref), channel_id=1, source_target_pairs={{0,24},{8,0},{16,8},{24,16},{32,56},{40,32},{48,40},{56,48},{64,88... | collective-permute-start | bytes 98312 | tf_op jit(solution)/shard_map/ppermute | solution.py:49
  65.3 5.1 %collective-permute-start.9 = (f32[32,256]{1,0:T(8,128)S(1)}, f32[32,256]{1,0:T(8,128)S(1)}, u32[]{:S(2)}, u32[]{:S(2)}) collective-permute-start(f32[32,256]{1,0:T(8,128)S(1)} %get-tuple-element.27.own_ref), channel_id=1, source_target_pairs={{0,16},{8,24},{16,0},{24,8},{32,48},{40,56},{48,32},{56,40},{64,80... | collective-permute-start | bytes 98312 | tf_op jit(solution)/shard_map/ppermute | solution.py:49
  70.5 15.8 %collective-permute-start.10 = (f32[32,256]{1,0:T(8,128)S(1)}, f32[32,256]{1,0:T(8,128)S(1)}, u32[]{:S(2)}, u32[]{:S(2)}) collective-permute-start(f32[32,256]{1,0:T(8,128)S(1)} %get-tuple-element.29.total_ref), channel_id=1, source_target_pairs={{0,32},{8,40},{16,48},{24,56},{32,0},{40,8},{48,16},{56,24},{64,96... | collective-permute-start | bytes 98312 | tf_op jit(solution)/shard_map/ppermute | solution.py:49
  86.3 7.4 %collective-permute-start.11 = (f32[32,256]{1,0:T(8,128)S(1)}, f32[32,256]{1,0:T(8,128)S(1)}, u32[]{:S(2)}, u32[]{:S(2)}) collective-permute-start(f32[32,256]{1,0:T(8,128)S(1)} %get-tuple-element.31.own_ref), channel_id=1, source_target_pairs={{0,64},{8,72},{16,80},{24,88},{32,96},{40,104},{48,112},{56,120},{... | collective-permute-start | bytes 98312 | tf_op jit(solution)/shard_map/ppermute | solution.py:49
  87.6 6.1 %collective-permute-start.12 = (f32[32,256]{1,0:T(8,128)S(1)}, f32[32,256]{1,0:T(8,128)S(1)}, u32[]{:S(2)}, u32[]{:S(2)}) collective-permute-start(f32[32,256]{1,0:T(8,128)S(1)} %get-tuple-element.31.own_ref), channel_id=1, source_target_pairs={{0,192},{8,200},{16,208},{24,216},{32,224},{40,232},{48,240},{56,2... | collective-permute-start | bytes 98312 | tf_op jit(solution)/shard_map/ppermute | solution.py:49
  89.9 6.7 %collective-permute-start.13 = (f32[32,256]{1,0:T(8,128)S(1)}, f32[32,256]{1,0:T(8,128)S(1)}, u32[]{:S(2)}, u32[]{:S(2)}) collective-permute-start(f32[32,256]{1,0:T(8,128)S(1)} %get-tuple-element.31.own_ref), channel_id=1, source_target_pairs={{0,128},{8,136},{16,144},{24,152},{32,160},{40,168},{48,176},{56,1... | collective-permute-start | bytes 98312 | tf_op jit(solution)/shard_map/ppermute | solution.py:49
  96.6 7.5 %collective-permute-start.14 = (f32[2,32,256]{2,1,0:T(8,128)S(1)}, f32[2,32,256]{2,1,0:T(8,128)S(1)}, u32[]{:S(2)}, u32[]{:S(2)}) collective-permute-start(f32[2,32,256]{2,1,0:T(8,128)S(1)} %shard_map.51.refs_0_), channel_id=1, source_target_pairs={{0,2},{1,3},{2,4},{3,5},{4,6},{5,7},{6,0},{7,1},{8,10},{9,11},{10,... | collective-permute-start | bytes 196616 | tf_op jit(solution)/shard_map/ppermute | solution.py:49
  97.6 8.7 %collective-permute-start.15 = (f32[2,32,256]{2,1,0:T(8,128)S(1)}, f32[2,32,256]{2,1,0:T(8,128)S(1)}, u32[]{:S(2)}, u32[]{:S(2)}) collective-permute-start(f32[2,32,256]{2,1,0:T(8,128)S(1)} %shard_map.51.refs_0_), channel_id=1, source_target_pairs={{0,6},{1,7},{2,0},{3,1},{4,2},{5,3},{6,4},{7,5},{8,14},{9,15},{10,... | collective-permute-start | bytes 196616 | tf_op jit(solution)/shard_map/ppermute | solution.py:49
  99.4 6.9 %collective-permute-start.16 = (f32[2,32,256]{2,1,0:T(8,128)S(1)}, f32[2,32,256]{2,1,0:T(8,128)S(1)}, u32[]{:S(2)}, u32[]{:S(2)}) collective-permute-start(f32[2,32,256]{2,1,0:T(8,128)S(1)} %shard_map.51.refs_0_), channel_id=1, source_target_pairs={{0,4},{1,5},{2,6},{3,7},{4,0},{5,1},{6,2},{7,3},{8,12},{9,13},{10,... | collective-permute-start | bytes 196616 | tf_op jit(solution)/shard_map/ppermute | solution.py:49
  99.4 12.6 %collective-permute-start.17 = (f32[2,32,256]{2,1,0:T(8,128)S(1)}, f32[2,32,256]{2,1,0:T(8,128)S(1)}, u32[]{:S(2)}, u32[]{:S(2)}) collective-permute-start(f32[2,32,256]{2,1,0:T(8,128)S(1)} %shard_map.51.refs_0_), channel_id=1, source_target_pairs={{0,1},{1,0},{2,3},{3,2},{4,5},{5,4},{6,7},{7,6},{8,9},{9,8},{10,11... | collective-permute-start | bytes 196616 | tf_op jit(solution)/shard_map/ppermute | solution.py:49
  104.1 7.9 %collective-permute-start.18 = (f32[2,32,256]{2,1,0:T(8,128)S(1)}, f32[2,32,256]{2,1,0:T(8,128)S(1)}, u32[]{:S(2)}, u32[]{:S(2)}) collective-permute-start(f32[2,32,256]{2,1,0:T(8,128)S(1)} %collective-permute-done.14.refs_1_), channel_id=1, source_target_pairs={{0,1},{1,0},{2,3},{3,2},{4,5},{5,4},{6,7},{7,6},{8,9},{9,8},{10,11... | collective-permute-start | bytes 196616 | tf_op jit(solution)/shard_map/ppermute | solution.py:49
  106.3 5.7 %collective-permute-start.19 = (f32[2,32,256]{2,1,0:T(8,128)S(1)}, f32[2,32,256]{2,1,0:T(8,128)S(1)}, u32[]{:S(2)}, u32[]{:S(2)}) collective-permute-start(f32[2,32,256]{2,1,0:T(8,128)S(1)} %collective-permute-done.15.refs_2_), channel_id=1, source_target_pairs={{0,1},{1,0},{2,3},{3,2},{4,5},{5,4},{6,7},{7,6},{8,9},{9,8},{10,11... | collective-permute-start | bytes 196616 | tf_op jit(solution)/shard_map/ppermute | solution.py:49
  106.3 5.7 %collective-permute-start.20 = (f32[2,32,256]{2,1,0:T(8,128)S(1)}, f32[2,32,256]{2,1,0:T(8,128)S(1)}, u32[]{:S(2)}, u32[]{:S(2)}) collective-permute-start(f32[2,32,256]{2,1,0:T(8,128)S(1)} %collective-permute-done.16.refs_3_), channel_id=1, source_target_pairs={{0,1},{1,0},{2,3},{3,2},{4,5},{5,4},{6,7},{7,6},{8,9},{9,8},{10,11... | collective-permute-start | bytes 196616 | tf_op jit(solution)/shard_map/ppermute | solution.py:49

commit v2 on v1

--- a/solution.py
+++ b/solution.py
@@ -33,6 +33,10 @@
     return dot(lh, rh, dims, default) + (dot(ll, rh, dims, default) + dot(lh, rl, dims, default))
 
 
+def dot4(left, right, dims=(1, 0)):
+    return dot3(left, right, dims) + dot(left[1], right[1], dims, lax.Precision.DEFAULT)
+
+
 def room(mebibytes):
     return pltpu.CompilerParams(vmem_limit_bytes=mebibytes * 2**20)
 
@@ -85,7 +89,7 @@
 
 
 def gather_kernel(panel_ref, *refs):
-    pieces, (high_ref, low_ref, gram_ref, whole_ref, own_ref, arrived) = refs[:-6], refs[-6:]
+    pieces, (high_ref, low_ref, gram_ref, own_ref, arrived) = refs[:-5], refs[-5:]
     height = own_ref.shape[0]
     fetch = pltpu.make_async_copy(panel_ref, own_ref, arrived)
     fetch.start()
@@ -93,7 +97,6 @@
 
     def place(value, owner):
         rows = pl.ds(pl.multiple_of(owner * height, height), height)
-        whole_ref[rows, :] = value
         high, low = halves(value)
         high_ref[rows, :] = high
         low_ref[rows, :] = low
@@ -102,7 +105,7 @@
         place(piece[...], owner)
     fetch.wait()
     place(own_ref[...], owners[0])
-    gram_ref[...] = dot(own_ref[...], whole_ref[...], (1, 1))
+    gram_ref[...] = dot4(halves(own_ref[...]), (high_ref[...], low_ref[...]), (1, 1))
 
 
 def gather(pieces):
@@ -113,7 +116,7 @@
         gather_kernel,
         in_specs=[pl.BlockSpec(memory_space=pl.ANY)] + [pl.BlockSpec(memory_space=pltpu.VMEM)] * (len(pieces) - 1),
         out_shape=[jax.ShapeDtypeStruct((a, b), t) for a, b, t in shapes],
-        scratch_shapes=[pltpu.VMEM((width, rows), F32), pltpu.VMEM((height, rows), F32), pltpu.SemaphoreType.DMA],
+        scratch_shapes=[pltpu.VMEM((height, rows), F32), pltpu.SemaphoreType.DMA],
         cost_estimate=cost(4),
         compiler_params=room(16),
         name="gather",
@@ -163,29 +166,13 @@
 
 
 def cross_kernel(high_ref, low_ref, right_high_ref, right_low_ref, out_ref):
-    product = dot3((high_ref[...], low_ref[...]), (right_high_ref[...], right_low_ref[...]))
-
-    @pl.when(pl.program_id(0) == 0)
-    def _():
-        out_ref[...] = product
-
-    @pl.when(pl.program_id(0) > 0)
-    def _():
-        out_ref[...] += product
+    out_ref[...] = dot3((high_ref[...], low_ref[...]), (right_high_ref[...], right_low_ref[...]))
 
 
 def cross(high, low, right_high, right_low):
-    width, rows = high.shape
-    columns = right_high.shape[1]
-    block = 1024
-    left = pl.BlockSpec((width, block), lambda i: (0, i))
-    right = pl.BlockSpec((block, columns), lambda i: (i, 0))
     return pl.pallas_call(
         cross_kernel,
-        grid=(rows // block,),
-        in_specs=[left, left, right, right],
-        out_specs=pl.BlockSpec((width, columns), lambda i: (0, 0)),
-        out_shape=jax.ShapeDtypeStruct((width, columns), F32),
+        out_shape=jax.ShapeDtypeStruct((high.shape[0], right_high.shape[1]), F32),
         cost_estimate=cost(4),
         compiler_params=room(16),
         name="cross",
@@ -356,14 +343,19 @@
     )(*pieces)
 
 
+def cut(rows):
+    sizes = [rows // 2] * 2
+    return [pl.ds(sum(sizes[:i]), size) for i, size in enumerate(sizes)]
+
+
 def project_kernel(sums_ref, *refs):
     (sh_from, sl_from, high_from, low_from, trailing_from, blocks_to, out_to), refs = refs[:7], refs[7:]
     sh_ref, sl_ref, high_ref, low_ref, trailing_ref, blocks_ref, out_ref, first, coming, going = refs
     stops, both, columns = sums_ref.shape
     height = both // 2
     rows = trailing_ref.shape[0]
-    chunks = coming.shape[0]
-    size = rows // chunks
+    parts = cut(rows)
+    chunks = len(parts)
     solves = [
         pltpu.make_async_copy(sh_from, sh_ref, first.at[0]),
         pltpu.make_async_copy(sl_from, sl_ref, first.at[1]),
@@ -371,8 +363,7 @@
     for copy in solves:
         copy.start()
     arrivals = []
-    for i in range(chunks):
-        part = pl.ds(i * size, size)
+    for i, part in enumerate(parts):
         arrivals.append(
             [
                 pltpu.make_async_copy(source.at[part], target.at[part], coming.at[i, k])
@@ -391,8 +382,7 @@
     blocks_ref[...] = dot3((sh_ref[0], sl_ref[0]), prefix)
     leaving = [pltpu.make_async_copy(blocks_ref, blocks_to, going.at[chunks])]
     leaving[0].start()
-    for i in range(chunks):
-        part = pl.ds(i * size, size)
+    for i, part in enumerate(parts):
         for copy in arrivals[i]:
             copy.wait()
         out_ref[part, :] = trailing_ref[part, :] - dot3((high_ref[part, :], low_ref[part, :]), coeffs)
@@ -405,7 +395,7 @@
 def project(solves, sums, high, low, trailing):
     rows, columns = trailing.shape
     width = high.shape[1]
-    chunks = 8
+    chunks = len(cut(rows))
     anywhere = pl.BlockSpec(memory_space=pl.ANY)
     return pl.pallas_call(
         project_kernel,

time: 135 us -> 132 us (0.978)
  Pallas kernels: 35.8 us -> 33.3 us
  transfers between devices with their start and end apart: 22 -> 22, of which waited for: 4 -> 4; matrix products, arithmetic and copies ran while one was open for 0% -> 0% of each run, Pallas kernels for 16% -> 17%
where the time goes in v2:
time: 132 us
  starting transfers between devices  49 us (37%)
  Pallas kernels  33.3 us (25%)
  blocking collectives  27.6 us (21%)
  waiting for transfers between devices  21.2 us (16%)
    ppermute x21, starting transfers between devices, rotate(): return lax.ppermute(value, axis, pairs)  43.9 us
    all_to_all x1, blocking collectives, exchange(): return lax.all_to_all(value, 'row', 0, 0, tiled=True)  27.6 us
    ppermute x21, waiting for transfers between devices, rotate(): return lax.ppermute(value, axis, pairs)  21.2 us
    pallas_call x1, Pallas kernels, factor(): pl.pallas_call(factor_kernel, out_shape=[jax.ShapeDtypeStruct((order, ord...  14.7 us
    pallas_call x1, Pallas kernels, project(): pl.pallas_call(project_kernel, in_specs=[pl.BlockSpec(memory_space=pltpu....  6.25 us
    all_to_all x1, starting transfers between devices, exchange(): return lax.all_to_all(value, 'row', 0, 0, tiled=True)  5.05 us
    pallas_call x1, Pallas kernels, halve(): pl.pallas_call(halve_kernel, grid=(rows // block,), in_specs=[spec], out_...  4.83 us
  transfers between devices with their start and end apart: 22, of which 4 were waited for; matrix products, arithmetic and copies ran while one was open for 0% of the time, Pallas kernels for 17%

profile of v2, /device:TPU:1, one launch (start us, length us, event | category | flops | bytes accessed | tf_op | source)
XLA Modules:
  0.0 131.9 jit_solution(10693829228177297534)
XLA Ops:
  0.6 2.2 %collective-permute-start = (f32[32,2048]{1,0:T(8,128)}, f32[32,2048]{1,0:T(8,128)S(1)}, u32[]{:S(2)}, u32[]{:S(2)}) collective-permute-start(f32[32,2048]{1,0:T(8,128)} %panel_ref.1), channel_id=1, source_target_pairs={{0,2},{1,3},{2,4},{3,5},{4,6},{5,7},{6,0},{7,1},{8,10},{9,11},{10,... | collective-permute-start | bytes 786440 | tf_op jit(solution)/shard_map/ppermute | solution.py:53
  2.8 1.5 %collective-permute-start.1 = (f32[32,2048]{1,0:T(8,128)}, f32[32,2048]{1,0:T(8,128)S(1)}, u32[]{:S(2)}, u32[]{:S(2)}) collective-permute-start(f32[32,2048]{1,0:T(8,128)} %panel_ref.1), channel_id=1, source_target_pairs={{0,6},{1,7},{2,0},{3,1},{4,2},{5,3},{6,4},{7,5},{8,14},{9,15},{10,... | collective-permute-start | bytes 786440 | tf_op jit(solution)/shard_map/ppermute | solution.py:53
  4.4 1.6 %collective-permute-start.2 = (f32[32,2048]{1,0:T(8,128)}, f32[32,2048]{1,0:T(8,128)S(1)}, u32[]{:S(2)}, u32[]{:S(2)}) collective-permute-start(f32[32,2048]{1,0:T(8,128)} %panel_ref.1), channel_id=1, source_target_pairs={{0,4},{1,5},{2,6},{3,7},{4,0},{5,1},{6,2},{7,3},{8,12},{9,13},{10,... | collective-permute-start | bytes 786440 | tf_op jit(solution)/shard_map/ppermute | solution.py:53
  5.9 1.5 %collective-permute-start.3 = (f32[32,2048]{1,0:T(8,128)}, f32[32,2048]{1,0:T(8,128)S(1)}, u32[]{:S(2)}, u32[]{:S(2)}) collective-permute-start(f32[32,2048]{1,0:T(8,128)} %panel_ref.1), channel_id=1, source_target_pairs={{0,1},{1,0},{2,3},{3,2},{4,5},{5,4},{6,7},{7,6},{8,9},{9,8},{10,11... | collective-permute-start | bytes 786440 | tf_op jit(solution)/shard_map/ppermute | solution.py:53
  7.4 1.1 collective-permute-done.refs_0_
  8.6 3.2 %collective-permute-start.4 = (f32[32,2048]{1,0:T(8,128)S(1)}, f32[32,2048]{1,0:T(8,128)S(1)}, u32[]{:S(2)}, u32[]{:S(2)}) collective-permute-start(f32[32,2048]{1,0:T(8,128)S(1)} %collective-permute-done.refs_0_), channel_id=1, source_target_pairs={{0,1},{1,0},{2,3},{3,2},{4,5},{5,4},{6,7},{7,6},{8,9},{9,8},{10,11... | collective-permute-start | bytes 786440 | tf_op jit(solution)/shard_map/ppermute | solution.py:53
  11.7 5.3 %collective-permute-start.5 = (f32[32,2048]{1,0:T(8,128)S(1)}, f32[32,2048]{1,0:T(8,128)S(1)}, u32[]{:S(2)}, u32[]{:S(2)}) collective-permute-start(f32[32,2048]{1,0:T(8,128)S(1)} %collective-permute-done.1.refs_1_), channel_id=1, source_target_pairs={{0,1},{1,0},{2,3},{3,2},{4,5},{5,4},{6,7},{7,6},{8,9},{9,8},{10,11... | collective-permute-start | bytes 786440 | tf_op jit(solution)/shard_map/ppermute | solution.py:53
  17.0 1.5 %collective-permute-start.6 = (f32[32,2048]{1,0:T(8,128)S(1)}, f32[32,2048]{1,0:T(8,128)S(1)}, u32[]{:S(2)}, u32[]{:S(2)}) collective-permute-start(f32[32,2048]{1,0:T(8,128)S(1)} %collective-permute-done.2.refs_2_), channel_id=1, source_target_pairs={{0,1},{1,0},{2,3},{3,2},{4,5},{5,4},{6,7},{7,6},{8,9},{9,8},{10,11... | collective-permute-start | bytes 786440 | tf_op jit(solution)/shard_map/ppermute | solution.py:53
  18.5 4.8 %halve.1 = (bf16[2048,512]{1,0:T(8,128)(2,1)S(1)}, bf16[2048,512]{1,0:T(8,128)(2,1)S(1)}) custom-call(f32[2048,512]{1,0:T(8,128)} %refs_4_.1), custom_call_target="tpu_custom_call" | custom-call | flops 1000000000 | bytes 2000000 | tf_op jit(solution)/shard_map/halve/pallas_call | solution.py:156
  23.4 2.4 %gather.1 = (bf16[256,2048]{1,0:T(8,128)(2,1)S(1)}, bf16[256,2048]{1,0:T(8,128)(2,1)S(1)}, f32[32,256]{1,0:T(8,128)S(1)}) custom-call(f32[32,2048]{1,0:T(8,128)} %panel_ref.1, f32[32,2048]{1,0:T(8,128)S(1)} %collective-permute-done.refs_0_, f32[32,2048]{1,0:T(8,128)S(1)} %collective-permute-done.1.refs_1_, f32[32,2048]{1,0:T(8,128)S(1)} %collective-permute-done.2.refs_2_, ...), custom_call_target="tpu_custom_call" | custom-call | flops 2000000000 | bytes 4000000 | tf_op jit(solution)/shard_map/gather/pallas_call | solution.py:115
  25.8 1.8 %cross.1 = f32[256,512]{1,0:T(8,128)S(1)} custom-call(bf16[256,2048]{1,0:T(8,128)(2,1)S(1)} %get-tuple-element.32.high_ref, bf16[256,2048]{1,0:T(8,128)(2,1)S(1)} %get-tuple-element.33.low_ref, bf16[2048,512]{1,0:T(8,128)(2,1)S(1)} %get-tuple-element.34.right_high_ref, bf16[2048,512]{1,0:T(8,128)(2,1)S(1)} %get-tuple-element.35.right_low_ref), custom_call_target="tpu_custom_call" | custom-call | flops 2000000000 | bytes 4000000 | tf_op jit(solution)/shard_map/cross/pallas_call | solution.py:173
  27.6 27.6 %all_to_all.10.pieces_ref = f32[32,8,512]{2,1,0:T(8,128)S(1)} all-to-all(f32[32,8,512]{2,1,0:T(8,128)S(1)} %bitcast.1), channel_id=1, replica_groups=mesh['row'=32,'col'=8] {'row'}, dimensions={0} | all-to-all | bytes 1048576 | tf_op jit(solution)/shard_map/all_to_all | solution.py:428
  55.1 1.1 scan.1
  56.2 5.1 %all-to-all-start.1 = ((f32[32,16,512]{2,1,0:T(8,128)}), f32[32,16,512]{2,1,0:T(8,128)S(1)}, u32[]{:S(2)}, u32[]{:S(2)}) async-start(f32[32,16,512]{2,1,0:T(8,128)} %scan.1), calls=%async_computation.1 | async-start | bytes 2097152 | tf_op jit(solution)/shard_map/all_to_all | solution.py:428
  61.3 1.3 collective-permute-start.7
  62.6 1.4 %collective-permute-start.8 = (f32[32,256]{1,0:T(8,128)S(1)}, f32[32,256]{1,0:T(8,128)S(1)}, u32[]{:S(2)}, u32[]{:S(2)}) collective-permute-start(f32[32,256]{1,0:T(8,128)S(1)} %get-tuple-element.27.own_ref), channel_id=1, source_target_pairs={{0,24},{8,0},{16,8},{24,16},{32,56},{40,32},{48,40},{56,48},{64,88... | collective-permute-start | bytes 98312 | tf_op jit(solution)/shard_map/ppermute | solution.py:53
  64.0 1.5 %collective-permute-start.9 = (f32[32,256]{1,0:T(8,128)S(1)}, f32[32,256]{1,0:T(8,128)S(1)}, u32[]{:S(2)}, u32[]{:S(2)}) collective-permute-start(f32[32,256]{1,0:T(8,128)S(1)} %get-tuple-element.27.own_ref), channel_id=1, source_target_pairs={{0,16},{8,24},{16,0},{24,8},{32,48},{40,56},{48,32},{56,40},{64,80... | collective-permute-start | bytes 98312 | tf_op jit(solution)/shard_map/ppermute | solution.py:53
  65.5 3.6 %collective-permute-done.9.two_ref = f32[32,256]{1,0:T(8,128)S(1)} collective-permute-done((f32[32,256]{1,0:T(8,128)S(1)}, f32[32,256]{1,0:T(8,128)S(1)}, u32[]{:S(2)}, u32[]{:S(2)}) %collective-permute-start.9) | collective-permute-done | bytes 32800 | tf_op jit(solution)/shard_map/ppermute | solution.py:53
  69.2 2.3 %collective-permute-start.10 = (f32[32,256]{1,0:T(8,128)S(1)}, f32[32,256]{1,0:T(8,128)S(1)}, u32[]{:S(2)}, u32[]{:S(2)}) collective-permute-start(f32[32,256]{1,0:T(8,128)S(1)} %get-tuple-element.29.total_ref), channel_id=1, source_target_pairs={{0,32},{8,40},{16,48},{24,56},{32,0},{40,8},{48,16},{56,24},{64,96... | collective-permute-start | bytes 98312 | tf_op jit(solution)/shard_map/ppermute | solution.py:53
  71.5 13.5 %collective-permute-done.10.other_ref = f32[32,256]{1,0:T(8,128)S(1)} collective-permute-done((f32[32,256]{1,0:T(8,128)S(1)}, f32[32,256]{1,0:T(8,128)S(1)}, u32[]{:S(2)}, u32[]{:S(2)}) %collective-permute-start.10) | collective-permute-done | bytes 32800 | tf_op jit(solution)/shard_map/ppermute | solution.py:53
  85.0 1.3 collective-permute-start.11
  86.3 2.3 %collective-permute-start.12 = (f32[32,256]{1,0:T(8,128)S(1)}, f32[32,256]{1,0:T(8,128)S(1)}, u32[]{:S(2)}, u32[]{:S(2)}) collective-permute-start(f32[32,256]{1,0:T(8,128)S(1)} %get-tuple-element.31.own_ref), channel_id=1, source_target_pairs={{0,192},{8,200},{16,208},{24,216},{32,224},{40,232},{48,240},{56,2... | collective-permute-start | bytes 98312 | tf_op jit(solution)/shard_map/ppermute | solution.py:53
  88.6 3.7 %collective-permute-start.13 = (f32[32,256]{1,0:T(8,128)S(1)}, f32[32,256]{1,0:T(8,128)S(1)}, u32[]{:S(2)}, u32[]{:S(2)}) collective-permute-start(f32[32,256]{1,0:T(8,128)S(1)} %get-tuple-element.31.own_ref), channel_id=1, source_target_pairs={{0,128},{8,136},{16,144},{24,152},{32,160},{40,168},{48,176},{56,1... | collective-permute-start | bytes 98312 | tf_op jit(solution)/shard_map/ppermute | solution.py:53
  92.3 2.9 %collective-permute-done.13.two_ref = f32[32,256]{1,0:T(8,128)S(1)} collective-permute-done((f32[32,256]{1,0:T(8,128)S(1)}, f32[32,256]{1,0:T(8,128)S(1)}, u32[]{:S(2)}, u32[]{:S(2)}) %collective-permute-start.13) | collective-permute-done | bytes 32800 | tf_op jit(solution)/shard_map/ppermute | solution.py:53
  95.3 0.9 collective-permute-start.14
  96.2 1.8 %collective-permute-start.15 = (f32[2,32,256]{2,1,0:T(8,128)S(1)}, f32[2,32,256]{2,1,0:T(8,128)S(1)}, u32[]{:S(2)}, u32[]{:S(2)}) collective-permute-start(f32[2,32,256]{2,1,0:T(8,128)S(1)} %shard_map.51.refs_0_), channel_id=1, source_target_pairs={{0,6},{1,7},{2,0},{3,1},{4,2},{5,3},{6,4},{7,5},{8,14},{9,15},{10,... | collective-permute-start | bytes 196616 | tf_op jit(solution)/shard_map/ppermute | solution.py:53
  98.1 4.7 %collective-permute-start.17 = (f32[2,32,256]{2,1,0:T(8,128)S(1)}, f32[2,32,256]{2,1,0:T(8,128)S(1)}, u32[]{:S(2)}, u32[]{:S(2)}) collective-permute-start(f32[2,32,256]{2,1,0:T(8,128)S(1)} %shard_map.51.refs_0_), channel_id=1, source_target_pairs={{0,1},{1,0},{2,3},{3,2},{4,5},{5,4},{6,7},{7,6},{8,9},{9,8},{10,11... | collective-permute-start | bytes 196616 | tf_op jit(solution)/shard_map/ppermute | solution.py:53
  102.8 2.2 %collective-permute-start.18 = (f32[2,32,256]{2,1,0:T(8,128)S(1)}, f32[2,32,256]{2,1,0:T(8,128)S(1)}, u32[]{:S(2)}, u32[]{:S(2)}) collective-permute-start(f32[2,32,256]{2,1,0:T(8,128)S(1)} %collective-permute-done.14.refs_1_), channel_id=1, source_target_pairs={{0,1},{1,0},{2,3},{3,2},{4,5},{5,4},{6,7},{7,6},{8,9},{9,8},{10,11... | collective-permute-start | bytes 196616 | tf_op jit(solution)/shard_map/ppermute | solution.py:53
  105.0 3.5 %collective-permute-start.20 = (f32[2,32,256]{2,1,0:T(8,128)S(1)}, f32[2,32,256]{2,1,0:T(8,128)S(1)}, u32[]{:S(2)}, u32[]{:S(2)}) collective-permute-start(f32[2,32,256]{2,1,0:T(8,128)S(1)} %collective-permute-done.16.refs_3_), channel_id=1, source_target_pairs={{0,1},{1,0},{2,3},{3,2},{4,5},{5,4},{6,7},{7,6},{8,9},{9,8},{10,11... | collective-permute-start | bytes 196616 | tf_op jit(solution)/shard_map/ppermute | solution.py:53
  108.5 2.2 %turn.1 = (bf16[2048,256]{1,0:T(8,128)(2,1)}, bf16[2048,256]{1,0:T(8,128)(2,1)}) custom-call(bf16[256,2048]{1,0:T(8,128)(2,1)S(1)} %get-tuple-element.32.high_ref, bf16[256,2048]{1,0:T(8,128)(2,1)S(1)} %get-tuple-element.33.low_ref), custom_call_target="tpu_custom_call" | custom-call | flops 1500000000 | bytes 3000000 | tf_op jit(solution)/shard_map/turn/pallas_call | solution.py:135
  110.7 14.7 %factor.1 = (f32[256,256]{1,0:T(8,128)}, bf16[2,256,256]{2,1,0:T(8,128)(2,1)}, bf16[2,256,256]{2,1,0:T(8,128)(2,1)}) custom-call(f32[2,32,256]{2,1,0:T(8,128)S(1)} %shard_map.51.refs_0_, f32[2,32,256]{2,1,0:T(8,128)S(1)} %collective-permute-done.14.refs_1_, f32[2,32,256]{2,1,0:T(8,128)S(1)} %collective-permute-done.15.refs_2_, ...), custom_call_target="tpu_custom_call" | custom-call | flops 8000000000 | bytes 16000000 | tf_op jit(solution)/shard_map/factor/pallas_call | solution.py:332
  125.5 6.2 %project.1 = (f32[256,512]{1,0:T(8,128)}, f32[2048,512]{1,0:T(8,128)}) custom-call(f32[32,16,512]{2,1,0:T(8,128)S(1)} %all-to-all-done.1.sums_ref, bf16[2,256,256]{2,1,0:T(8,128)(2,1)} %get-tuple-element.45.refs_0_, bf16[2,256,256]{2,1,0:T(8,128)(2,1)} %get-tuple-element.46.refs_1_, bf16[2048,256]{1,0:T(8,128)(2,1)} %get-tuple-element.47.refs_2_, ...), custom_call_target="tpu_custom_call" | custom-call | flops 3000000000 | bytes 6000000 | tf_op jit(solution)/shard_map/project/pallas_call | solution.py:400
  (23 shorter events, 0.2 us)
Async XLA Ops:
  0.6 7.9 %collective-permute-start = (f32[32,2048]{1,0:T(8,128)}, f32[32,2048]{1,0:T(8,128)S(1)}, u32[]{:S(2)}, u32[]{:S(2)}) collective-permute-start(f32[32,2048]{1,0:T(8,128)} %panel_ref.1), channel_id=1, source_target_pairs={{0,2},{1,3},{2,4},{3,5},{4,6},{5,7},{6,0},{7,1},{8,10},{9,11},{10,... | collective-permute-start | bytes 786440 | tf_op jit(solution)/shard_map/ppermute | solution.py:53
  2.8 8.9 %collective-permute-start.1 = (f32[32,2048]{1,0:T(8,128)}, f32[32,2048]{1,0:T(8,128)S(1)}, u32[]{:S(2)}, u32[]{:S(2)}) collective-permute-start(f32[32,2048]{1,0:T(8,128)} %panel_ref.1), channel_id=1, source_target_pairs={{0,6},{1,7},{2,0},{3,1},{4,2},{5,3},{6,4},{7,5},{8,14},{9,15},{10,... | collective-permute-start | bytes 786440 | tf_op jit(solution)/shard_map/ppermute | solution.py:53
  4.4 12.7 %collective-permute-start.2 = (f32[32,2048]{1,0:T(8,128)}, f32[32,2048]{1,0:T(8,128)S(1)}, u32[]{:S(2)}, u32[]{:S(2)}) collective-permute-start(f32[32,2048]{1,0:T(8,128)} %panel_ref.1), channel_id=1, source_target_pairs={{0,4},{1,5},{2,6},{3,7},{4,0},{5,1},{6,2},{7,3},{8,12},{9,13},{10,... | collective-permute-start | bytes 786440 | tf_op jit(solution)/shard_map/ppermute | solution.py:53
  5.9 17.5 %collective-permute-start.3 = (f32[32,2048]{1,0:T(8,128)}, f32[32,2048]{1,0:T(8,128)S(1)}, u32[]{:S(2)}, u32[]{:S(2)}) collective-permute-start(f32[32,2048]{1,0:T(8,128)} %panel_ref.1), channel_id=1, source_target_pairs={{0,1},{1,0},{2,3},{3,2},{4,5},{5,4},{6,7},{7,6},{8,9},{9,8},{10,11... | collective-permute-start | bytes 786440 | tf_op jit(solution)/shard_map/ppermute | solution.py:53
  8.6 14.8 %collective-permute-start.4 = (f32[32,2048]{1,0:T(8,128)S(1)}, f32[32,2048]{1,0:T(8,128)S(1)}, u32[]{:S(2)}, u32[]{:S(2)}) collective-permute-start(f32[32,2048]{1,0:T(8,128)S(1)} %collective-permute-done.refs_0_), channel_id=1, source_target_pairs={{0,1},{1,0},{2,3},{3,2},{4,5},{5,4},{6,7},{7,6},{8,9},{9,8},{10,11... | collective-permute-start | bytes 786440 | tf_op jit(solution)/shard_map/ppermute | solution.py:53
  11.7 11.7 %collective-permute-start.5 = (f32[32,2048]{1,0:T(8,128)S(1)}, f32[32,2048]{1,0:T(8,128)S(1)}, u32[]{:S(2)}, u32[]{:S(2)}) collective-permute-start(f32[32,2048]{1,0:T(8,128)S(1)} %collective-permute-done.1.refs_1_), channel_id=1, source_target_pairs={{0,1},{1,0},{2,3},{3,2},{4,5},{5,4},{6,7},{7,6},{8,9},{9,8},{10,11... | collective-permute-start | bytes 786440 | tf_op jit(solution)/shard_map/ppermute | solution.py:53
  17.0 6.4 %collective-permute-start.6 = (f32[32,2048]{1,0:T(8,128)S(1)}, f32[32,2048]{1,0:T(8,128)S(1)}, u32[]{:S(2)}, u32[]{:S(2)}) collective-permute-start(f32[32,2048]{1,0:T(8,128)S(1)} %collective-permute-done.2.refs_2_), channel_id=1, source_target_pairs={{0,1},{1,0},{2,3},{3,2},{4,5},{5,4},{6,7},{7,6},{8,9},{9,8},{10,11... | collective-permute-start | bytes 786440 | tf_op jit(solution)/shard_map/ppermute | solution.py:53
  56.2 69.3 %all-to-all-start.1 = ((f32[32,16,512]{2,1,0:T(8,128)}), f32[32,16,512]{2,1,0:T(8,128)S(1)}, u32[]{:S(2)}, u32[]{:S(2)}) async-start(f32[32,16,512]{2,1,0:T(8,128)} %scan.1), calls=%async_computation.1 | async-start | bytes 2097152 | tf_op jit(solution)/shard_map/all_to_all | solution.py:428
  61.3 4.3 %collective-permute-start.7 = (f32[32,256]{1,0:T(8,128)S(1)}, f32[32,256]{1,0:T(8,128)S(1)}, u32[]{:S(2)}, u32[]{:S(2)}) collective-permute-start(f32[32,256]{1,0:T(8,128)S(1)} %get-tuple-element.27.own_ref), channel_id=1, source_target_pairs={{0,8},{8,16},{16,24},{24,0},{32,40},{40,48},{48,56},{56,32},{64,72... | collective-permute-start | bytes 98312 | tf_op jit(solution)/shard_map/ppermute | solution.py:53
  62.6 3.0 %collective-permute-start.8 = (f32[32,256]{1,0:T(8,128)S(1)}, f32[32,256]{1,0:T(8,128)S(1)}, u32[]{:S(2)}, u32[]{:S(2)}) collective-permute-start(f32[32,256]{1,0:T(8,128)S(1)} %get-tuple-element.27.own_ref), channel_id=1, source_target_pairs={{0,24},{8,0},{16,8},{24,16},{32,56},{40,32},{48,40},{56,48},{64,88... | collective-permute-start | bytes 98312 | tf_op jit(solution)/shard_map/ppermute | solution.py:53
  64.0 5.1 %collective-permute-start.9 = (f32[32,256]{1,0:T(8,128)S(1)}, f32[32,256]{1,0:T(8,128)S(1)}, u32[]{:S(2)}, u32[]{:S(2)}) collective-permute-start(f32[32,256]{1,0:T(8,128)S(1)} %get-tuple-element.27.own_ref), channel_id=1, source_target_pairs={{0,16},{8,24},{16,0},{24,8},{32,48},{40,56},{48,32},{56,40},{64,80... | collective-permute-start | bytes 98312 | tf_op jit(solution)/shard_map/ppermute | solution.py:53
  69.2 15.8 %collective-permute-start.10 = (f32[32,256]{1,0:T(8,128)S(1)}, f32[32,256]{1,0:T(8,128)S(1)}, u32[]{:S(2)}, u32[]{:S(2)}) collective-permute-start(f32[32,256]{1,0:T(8,128)S(1)} %get-tuple-element.29.total_ref), channel_id=1, source_target_pairs={{0,32},{8,40},{16,48},{24,56},{32,0},{40,8},{48,16},{56,24},{64,96... | collective-permute-start | bytes 98312 | tf_op jit(solution)/shard_map/ppermute | solution.py:53
  85.0 7.4 %collective-permute-start.11 = (f32[32,256]{1,0:T(8,128)S(1)}, f32[32,256]{1,0:T(8,128)S(1)}, u32[]{:S(2)}, u32[]{:S(2)}) collective-permute-start(f32[32,256]{1,0:T(8,128)S(1)} %get-tuple-element.31.own_ref), channel_id=1, source_target_pairs={{0,64},{8,72},{16,80},{24,88},{32,96},{40,104},{48,112},{56,120},{... | collective-permute-start | bytes 98312 | tf_op jit(solution)/shard_map/ppermute | solution.py:53
  86.3 6.1 %collective-permute-start.12 = (f32[32,256]{1,0:T(8,128)S(1)}, f32[32,256]{1,0:T(8,128)S(1)}, u32[]{:S(2)}, u32[]{:S(2)}) collective-permute-start(f32[32,256]{1,0:T(8,128)S(1)} %get-tuple-element.31.own_ref), channel_id=1, source_target_pairs={{0,192},{8,200},{16,208},{24,216},{32,224},{40,232},{48,240},{56,2... | collective-permute-start | bytes 98312 | tf_op jit(solution)/shard_map/ppermute | solution.py:53
  88.6 6.7 %collective-permute-start.13 = (f32[32,256]{1,0:T(8,128)S(1)}, f32[32,256]{1,0:T(8,128)S(1)}, u32[]{:S(2)}, u32[]{:S(2)}) collective-permute-start(f32[32,256]{1,0:T(8,128)S(1)} %get-tuple-element.31.own_ref), channel_id=1, source_target_pairs={{0,128},{8,136},{16,144},{24,152},{32,160},{40,168},{48,176},{56,1... | collective-permute-start | bytes 98312 | tf_op jit(solution)/shard_map/ppermute | solution.py:53
  95.3 7.5 %collective-permute-start.14 = (f32[2,32,256]{2,1,0:T(8,128)S(1)}, f32[2,32,256]{2,1,0:T(8,128)S(1)}, u32[]{:S(2)}, u32[]{:S(2)}) collective-permute-start(f32[2,32,256]{2,1,0:T(8,128)S(1)} %shard_map.51.refs_0_), channel_id=1, source_target_pairs={{0,2},{1,3},{2,4},{3,5},{4,6},{5,7},{6,0},{7,1},{8,10},{9,11},{10,... | collective-permute-start | bytes 196616 | tf_op jit(solution)/shard_map/ppermute | solution.py:53
  96.2 8.7 %collective-permute-start.15 = (f32[2,32,256]{2,1,0:T(8,128)S(1)}, f32[2,32,256]{2,1,0:T(8,128)S(1)}, u32[]{:S(2)}, u32[]{:S(2)}) collective-permute-start(f32[2,32,256]{2,1,0:T(8,128)S(1)} %shard_map.51.refs_0_), channel_id=1, source_target_pairs={{0,6},{1,7},{2,0},{3,1},{4,2},{5,3},{6,4},{7,5},{8,14},{9,15},{10,... | collective-permute-start | bytes 196616 | tf_op jit(solution)/shard_map/ppermute | solution.py:53
  98.1 6.9 %collective-permute-start.16 = (f32[2,32,256]{2,1,0:T(8,128)S(1)}, f32[2,32,256]{2,1,0:T(8,128)S(1)}, u32[]{:S(2)}, u32[]{:S(2)}) collective-permute-start(f32[2,32,256]{2,1,0:T(8,128)S(1)} %shard_map.51.refs_0_), channel_id=1, source_target_pairs={{0,4},{1,5},{2,6},{3,7},{4,0},{5,1},{6,2},{7,3},{8,12},{9,13},{10,... | collective-permute-start | bytes 196616 | tf_op jit(solution)/shard_map/ppermute | solution.py:53
  98.1 12.6 %collective-permute-start.17 = (f32[2,32,256]{2,1,0:T(8,128)S(1)}, f32[2,32,256]{2,1,0:T(8,128)S(1)}, u32[]{:S(2)}, u32[]{:S(2)}) collective-permute-start(f32[2,32,256]{2,1,0:T(8,128)S(1)} %shard_map.51.refs_0_), channel_id=1, source_target_pairs={{0,1},{1,0},{2,3},{3,2},{4,5},{5,4},{6,7},{7,6},{8,9},{9,8},{10,11... | collective-permute-start | bytes 196616 | tf_op jit(solution)/shard_map/ppermute | solution.py:53
  102.8 7.9 %collective-permute-start.18 = (f32[2,32,256]{2,1,0:T(8,128)S(1)}, f32[2,32,256]{2,1,0:T(8,128)S(1)}, u32[]{:S(2)}, u32[]{:S(2)}) collective-permute-start(f32[2,32,256]{2,1,0:T(8,128)S(1)} %collective-permute-done.14.refs_1_), channel_id=1, source_target_pairs={{0,1},{1,0},{2,3},{3,2},{4,5},{5,4},{6,7},{7,6},{8,9},{9,8},{10,11... | collective-permute-start | bytes 196616 | tf_op jit(solution)/shard_map/ppermute | solution.py:53
  105.0 5.7 %collective-permute-start.19 = (f32[2,32,256]{2,1,0:T(8,128)S(1)}, f32[2,32,256]{2,1,0:T(8,128)S(1)}, u32[]{:S(2)}, u32[]{:S(2)}) collective-permute-start(f32[2,32,256]{2,1,0:T(8,128)S(1)} %collective-permute-done.15.refs_2_), channel_id=1, source_target_pairs={{0,1},{1,0},{2,3},{3,2},{4,5},{5,4},{6,7},{7,6},{8,9},{9,8},{10,11... | collective-permute-start | bytes 196616 | tf_op jit(solution)/shard_map/ppermute | solution.py:53
  105.0 5.7 %collective-permute-start.20 = (f32[2,32,256]{2,1,0:T(8,128)S(1)}, f32[2,32,256]{2,1,0:T(8,128)S(1)}, u32[]{:S(2)}, u32[]{:S(2)}) collective-permute-start(f32[2,32,256]{2,1,0:T(8,128)S(1)} %collective-permute-done.16.refs_3_), channel_id=1, source_target_pairs={{0,1},{1,0},{2,3},{3,2},{4,5},{5,4},{6,7},{7,6},{8,9},{9,8},{10,11... | collective-permute-start | bytes 196616 | tf_op jit(solution)/shard_map/ppermute | solution.py:53
